TPU v7x, 256 devices: a whole 4x4x8 slice. The times are simulated.
256 devices in a mesh: dp: 128 (over y, z, x), tensor: 2 (over core).
Axes of the slice: x: 4, y: 4, z: 8, core: 2. Of those that a mesh axis runs over, the one named last changes fastest.
Arguments:
- fc_grads: bfloat16 [128, 768, 3072], P('dp', None, 'tensor')
- fc_error: bfloat16 [128, 768, 3072], P('dp', None, 'tensor'), may hold values from -4 to 4
- query: float32 [3072, 32], P('tensor'), may hold values from -0.109375 to 0.109375
- gram_inverse: float32 [32, 32], replicated
- fc_master: float32 [768, 3072], P('dp', 'tensor'), may hold values from -6 to 6
- fc_momentum: float32 [768, 3072], P('dp', 'tensor'), may hold values from -3 to 3
- vec_grads: bfloat16 [128, 5376], P('dp'), may hold values from -24 to 24
- vec_master: float32 [5376], P('dp'), may hold values from -6 to 6
- vec_momentum: float32 [5376], P('dp'), may hold values from -4 to 4
Outputs:
- new_error: bfloat16 [128, 768, 3072], P('dp', None, 'tensor')
- new_momentum: float32 [768, 3072], P('dp', 'tensor')
- new_master: float32 [768, 3072], P('dp', 'tensor')
- new_weights: bfloat16 [768, 3072], P(None, 'tensor')
- vec_new_momentum: float32 [5376], P('dp')
- vec_new_master: float32 [5376], P('dp')
- vec_weights: bfloat16 [5376], replicated
All inputs are finite; a program needn't handle non-finite values.
Results may differ from a plain program's by a relative error of at most 0.0085.
Values may be sent and summed in bfloat16 or wider, within the bound.
No kernel may reach another device: no remote copies, remote signals or barrier semaphores. Data moves between devices by JAX's collectives and lax.ppermute only.
A program may use at most 64 MiB of HBM per device.

v0:
```python
import jax
import jax.numpy as jnp
from jax import lax
from jax.sharding import PartitionSpec as P

momentum_decay = 0.9
step_size = 0.5


def on_device(
    fc_grads,
    fc_error,
    query,
    gram_inverse,
    fc_master,
    fc_momentum,
    vec_grads,
    vec_master,
    vec_momentum,
):
    replicas = lax.axis_size("dp")
    replica_index = lax.axis_index("dp")
    merged = (fc_grads[0].astype(jnp.float32) + fc_error[0].astype(jnp.float32)).astype(
        jnp.bfloat16
    )
    query_b = query.astype(jnp.bfloat16)
    row_part = jnp.dot(merged, query_b, preferred_element_type=jnp.float32)
    vec_term = vec_grads[0].astype(jnp.float32)
    shard_len = vec_master.shape[0]
    row_total = lax.psum(row_part, ("dp", "tensor"))
    vec_total = lax.psum(vec_term, "dp")
    vec_mean = (
        lax.dynamic_slice_in_dim(vec_total, replica_index * shard_len, shard_len, 0) / replicas
    )
    row_mean = row_total / replicas
    row_basis = jnp.dot(row_mean, gram_inverse, precision=lax.Precision.HIGHEST)
    basis_b = row_basis.astype(jnp.bfloat16)
    col_part = lax.dot_general(
        merged, basis_b, (((0,), (0,)), ((), ())), preferred_element_type=jnp.float32
    )
    col_mean = lax.psum(col_part, "dp") / replicas
    approx = jnp.dot(row_basis, col_mean.T, precision=lax.Precision.HIGHEST)
    new_error = (merged.astype(jnp.float32) - approx).astype(jnp.bfloat16)[None]
    state_rows = fc_master.shape[0]
    basis_rows = lax.dynamic_slice_in_dim(row_basis, replica_index * state_rows, state_rows, 0)
    approx_rows = jnp.dot(basis_rows, col_mean.T, precision=lax.Precision.HIGHEST)
    new_momentum = momentum_decay * fc_momentum + approx_rows
    new_master = fc_master - step_size * (approx_rows + momentum_decay * new_momentum)
    vec_new_momentum = momentum_decay * vec_momentum + vec_mean
    vec_new_master = vec_master - step_size * (vec_mean + momentum_decay * vec_new_momentum)
    new_weights, vec_weights = (
        lax.all_gather(new_master.astype(jnp.bfloat16), "dp", axis=0, tiled=True),
        lax.all_gather(vec_new_master.astype(jnp.bfloat16), "dp", axis=0, tiled=True),
    )
    return (
        new_error,
        new_momentum,
        new_master,
        new_weights,
        vec_new_momentum,
        vec_new_master,
        vec_weights,
    )


def solution(mesh):
    return jax.shard_map(
        on_device,
        mesh=mesh,
        in_specs=(
            P("dp", None, "tensor"),
            P("dp", None, "tensor"),
            P("tensor", None),
            P(),
            P("dp", "tensor"),
            P("dp", "tensor"),
            P("dp", None),
            P("dp"),
            P("dp"),
        ),
        out_specs=(
            P("dp", None, "tensor"),
            P("dp", "tensor"),
            P("dp", "tensor"),
            P(None, "tensor"),
            P("dp"),
            P("dp"),
            P(),
        ),
        check_vma=False,
    )
```

profile of v0, /device:TPU:32, one launch (start us, length us, event | category | flops | bytes accessed | tf_op | source)
XLA Modules:
  0.0 1851.5 jit_solution(18031364214805871848)
XLA Ops:
  7.2 0.0 copy-start
  7.2 0.0 copy-start.1
  7.2 0.0 all-reduce.4.cloned.1.call-start
  7.2 4.0 fusion.9
  11.2 0.0 all-reduce.4.cloned.1.call-update
  11.2 0.0 all-reduce.6.cloned.1.call-start
  11.3 244.5 %all-reduce.4.cloned.1.call-done = f32[768,32]{0,1:T(8,128)} async-done(((f32[768,32]{0,1:T(8,128)}), f32[768,32]{0,1:T(8,128)}) %all-reduce.4.cloned.1.call-update) | async-done | bytes 98320 | tf_op jit(solution)/shard_map/psum | solution.py:30
  255.8 0.0 copy-done
  255.8 1.2 fusion.7
  257.0 0.0 copy-done.1
  257.0 0.0 copy-start.2
  257.0 0.0 copy-start.3
  257.0 0.0 copy-start.7
  257.0 0.0 copy-start.4
  257.1 0.0 copy-start.5
  257.1 0.0 copy-start.6
  257.1 3.1 fusion.11
  260.2 0.0 all-reduce.6.cloned.1.call-update
  260.2 0.0 all-gather.3.cloned.1.call-start
  260.3 210.3 %all-reduce.6.cloned.1.call-done = f32[1536,32]{0,1:T(8,128)} async-done(((f32[1536,32]{0,1:T(8,128)}), f32[1536,32]{0,1:T(8,128)}) %all-reduce.6.cloned.1.call-update) | async-done | bytes 196624 | tf_op jit(solution)/shard_map/psum | solution.py:41
  470.5 0.0 copy-done.2
  470.5 0.0 copy-done.3
  470.5 1.9 convert_bitcast_fusion
  472.4 0.0 all-gather.3.cloned.1.call-update
  472.5 0.0 copy-done.7
  472.5 0.6 dynamic-slice
  473.7 0.0 copy-done.4
  473.7 0.1 convert_reduce_fusion
  473.8 677.0 %psum.23 = f32[5376]{0:T(1024)S(1)} all-reduce(f32[5376]{0:T(1024)S(1)} %convert_reduce_fusion), channel_id=1, replica_groups=mesh['dp'=128,'tensor'=2] {'dp'}, use_global_device_ids=true, to_apply=%region_2.0 | all-reduce | flops 5376 | bytes 43008 | tf_op jit(solution)/shard_map/psum | solution.py:31
  1150.8 0.0 copy-done.5
  1150.8 0.0 copy-done.6
  1150.8 0.6 fusion.21
  1151.4 0.2 dynamic-update-slice
  1151.6 681.7 %all-reduce = bf16[5376]{0:T(1024)(128)(2,1)} all-reduce(bf16[5376]{0:T(1024)(128)(2,1)S(1)} %dynamic-update-slice), channel_id=1, replica_groups=mesh['dp'=128,'tensor'=2] {'dp'}, use_global_device_ids=true, to_apply=%add | all-reduce | flops 5376 | bytes 21504
  1833.3 6.6 fusion
  1839.9 0.0 all-gather.3.cloned.1.call-done
  1839.9 5.0 reshape.25
  (1 shorter events, 0.0 us)
Async XLA Ops:
  7.2 248.7 %copy-start = (f32[32,32]{1,0:T(8,128)S(1)}, f32[32,32]{1,0:T(8,128)}, u32[]{:S(2)}) copy-start(f32[32,32]{1,0:T(8,128)} %param.12) | copy-start | bytes 12292
  7.2 249.8 %copy-start.1 = (bf16[1,768,1536]{2,1,0:T(8,128)(2,1)S(1)}, bf16[1,768,1536]{2,1,0:T(8,128)(2,1)}, u32[]{:S(2)}) copy-start(bf16[1,768,1536]{2,1,0:T(8,128)(2,1)} %param.10) | copy-start | bytes 7077892
  7.2 248.6 %all-reduce.4.cloned.1.call-start = ((), (), s32[]{:S(2)}) async-start(), calls=%async_computation | async-start | bytes 196608 | tf_op jit(solution)/shard_map/psum | solution.py:30
  11.2 459.3 %all-reduce.6.cloned.1.call-start = ((), (), s32[]{:S(2)}) async-start(), calls=%async_computation.1 | async-start | bytes 393216 | tf_op jit(solution)/shard_map/psum | solution.py:41
  257.0 213.5 %copy-start.2 = (f32[6,1536]{1,0:T(8,128)S(1)}, f32[6,1536]{1,0:T(8,128)}, u32[]{:S(2)}) copy-start(f32[6,1536]{1,0:T(8,128)} %param.13) | copy-start | bytes 110596
  257.0 213.5 %copy-start.3 = (f32[6,1536]{1,0:T(8,128)S(1)}, f32[6,1536]{1,0:T(8,128)}, u32[]{:S(2)}) copy-start(f32[6,1536]{1,0:T(8,128)} %param.14) | copy-start | bytes 110596
  257.0 215.4 %copy-start.7 = (u32[256]{0:T(256)S(1)}, u32[256]{0:T(256)}, u32[]{:S(2)}) copy-start(u32[256]{0:T(256)} %constant.38) | copy-start | bytes 3076
  257.0 216.7 %copy-start.4 = (bf16[1,5376]{1,0:T(2,128)(2,1)S(1)}, bf16[1,5376]{1,0:T(2,128)(2,1)}, u32[]{:S(2)}) copy-start(bf16[1,5376]{1,0:T(2,128)(2,1)} %param.15) | copy-start | bytes 32260
  257.1 893.7 %copy-start.5 = (f32[42]{0:T(128)S(1)}, f32[42]{0:T(128)}, u32[]{:S(2)}) copy-start(f32[42]{0:T(128)} %param.16) | copy-start | bytes 508
  257.1 893.7 %copy-start.6 = (f32[42]{0:T(128)S(1)}, f32[42]{0:T(128)}, u32[]{:S(2)}) copy-start(f32[42]{0:T(128)} %param.17) | copy-start | bytes 508
  260.2 1579.7 %all-gather.3.cloned.1.call-start = ((), (), s32[]{:S(2)}) async-start(), calls=%async_computation.2 | async-start | bytes 3170304 | tf_op jit(solution)/shard_map/all_gather | solution.py:52
Sparse Core Ops, SparseCore 0:
  14.1 241.6 all-reduce.3
  261.8 208.6 all-reduce.5
  475.4 112.8 all-gather.2
where the time goes:
time: 1860 us; the launch traced here: 1850 us
  blocking collectives  1360 us (73%)
  waiting for transfers between devices  455 us (24%)
    unnamed x1, blocking collectives  682 us
    psum x1, blocking collectives, on_device(): vec_total = lax.psum(vec_term, 'dp')  677 us
    psum x1, waiting for transfers between devices, on_device(): row_total = lax.psum(row_part, ('dp', 'tensor'))  245 us
    psum x1, waiting for transfers between devices, on_device(): col_mean = lax.psum(col_part, 'dp') / replicas  210 us
  transfers between devices with their start and end apart: 3, of which 2 were waited for; matrix products, arithmetic and copies ran while one was open for 0% of the time, Pallas kernels for 0%

commit v1 on v0

v1 whole, which is shorter than its diff:
```python
import jax
import jax.numpy as jnp
from jax import lax
from jax.sharding import Mesh, PartitionSpec as P

momentum_decay = 0.9
step_size = 0.5
SIZES = {"y": 4, "z": 8, "x": 4, "c": 2}
LANES = 128


def exchange(value, axis):
    n = SIZES[axis]
    return [value] + [lax.ppermute(value, axis, [(i, i ^ d) for i in range(n)]) for d in range(1, n)]


def in_order(blocks, index):
    bit = 1
    while bit < len(blocks):
        swap = (index & bit) != 0
        blocks = [jnp.where(swap, blocks[j ^ bit], blocks[j]) for j in range(len(blocks))]
        bit *= 2
    return blocks


def total(blocks):
    while len(blocks) > 1:
        blocks = [blocks[j] + blocks[j + 1] for j in range(0, len(blocks), 2)]
    return blocks[0]


def on_device(
    fc_grads,
    fc_error,
    query,
    gram_inverse,
    fc_master,
    fc_momentum,
    vec_grads,
    vec_master,
    vec_momentum,
):
    x, y, z, c = (lax.axis_index(a) for a in "xyzc")
    replica_index = (y * SIZES["z"] + z) * SIZES["x"] + x
    replicas = SIZES["y"] * SIZES["z"] * SIZES["x"]
    merged = (fc_grads[0].astype(jnp.float32) + fc_error[0].astype(jnp.float32)).astype(
        jnp.bfloat16
    )
    query_b = query.astype(jnp.bfloat16)
    row_part = lax.dot_general(
        query_b, merged, (((0,), (1,)), ((), ())), preferred_element_type=jnp.float32
    )
    rank, width = row_part.shape
    half = rank // 2
    row_half = lax.dynamic_slice_in_dim(row_part, c * half, half, 0)
    row_other = lax.dynamic_slice_in_dim(row_part, (1 - c) * half, half, 0)
    row_half = row_half + lax.ppermute(row_other, "c", [(0, 1), (1, 0)])

    vec_len = vec_grads.shape[1]
    shard_len = vec_master.shape[0]
    vec_half = lax.dynamic_slice_in_dim(
        vec_grads[0].astype(jnp.float32), c * (vec_len // 2), vec_len // 2, 0
    )
    vec_base = lax.dynamic_update_slice_in_dim(
        jnp.zeros((vec_len,), jnp.float32),
        vec_master - step_size * momentum_decay * momentum_decay * vec_momentum,
        replica_index * shard_len,
        0,
    )
    vec_base = lax.dynamic_slice_in_dim(vec_base, c * (vec_len // 2), vec_len // 2, 0)
    base = fc_master - step_size * momentum_decay * momentum_decay * fc_momentum

    sums = jnp.concatenate([v.reshape(-1, LANES) for v in (row_half, vec_half, vec_base)], 0)
    n_sums = sums.shape[0]
    base = base.reshape(-1, LANES)
    for axis, index in (("x", x), ("y", y)):
        blocks = exchange(jnp.concatenate([sums, base], 0), axis)
        sums = total([b[:n_sums] for b in blocks])
        base = jnp.concatenate(in_order([b[n_sums:] for b in blocks], index), 0)
    base_all = lax.all_gather(base, "z", axis=0)
    sums = total(exchange(sums, "z"))
    sums = in_order(exchange(sums, "c"), c)
    n_row = half * width // LANES
    n_vec = vec_len // 2 // LANES
    row_total = jnp.concatenate([s[:n_row].reshape(half, width) for s in sums], 0)
    vec_total = jnp.concatenate([s[n_row : n_row + n_vec].reshape(-1) for s in sums], 0)
    vec_base = jnp.concatenate([s[n_row + n_vec :].reshape(-1) for s in sums], 0)

    row_basis = lax.dot_general(
        gram_inverse,
        row_total / replicas,
        (((0,), (0,)), ((), ())),
        precision=lax.Precision.HIGHEST,
    )
    basis_b = row_basis.astype(jnp.bfloat16)
    col_part = jnp.dot(basis_b, merged, preferred_element_type=jnp.float32)
    cols = col_part.shape[1]
    plane = SIZES["z"] * SIZES["x"]
    pieces = col_part.reshape(plane, -1, LANES)
    pieces = lax.all_to_all(pieces, ("z", "x"), 0, 0, tiled=True)
    piece = total(exchange(jnp.sum(pieces, 0), "y"))
    pieces = jnp.broadcast_to(piece[None], (plane,) + piece.shape)
    pieces = lax.all_to_all(pieces, ("z", "x"), 0, 0, tiled=True)
    col_mean = pieces.reshape(rank, cols) / replicas

    approx = lax.dot_general(
        row_basis, col_mean, (((0,), (0,)), ((), ())), precision=lax.Precision.HIGHEST
    )
    new_error = (merged.astype(jnp.float32) - approx).astype(jnp.bfloat16)[None]
    gain = step_size * (1.0 + momentum_decay)
    ny, nz = SIZES["y"], SIZES["z"]
    base_all = base_all.reshape(nz, ny, -1, cols).swapaxes(0, 1).reshape(width, cols)
    new_weights = (base_all - gain * approx).astype(jnp.bfloat16)

    state_rows = fc_master.shape[0]
    basis_rows = lax.dynamic_slice_in_dim(row_basis, replica_index * state_rows, state_rows, 1)
    approx_rows = lax.dot_general(
        basis_rows, col_mean, (((0,), (0,)), ((), ())), precision=lax.Precision.HIGHEST
    )
    new_momentum = momentum_decay * fc_momentum + approx_rows
    new_master = fc_master - step_size * (approx_rows + momentum_decay * new_momentum)

    vec_total = vec_total / replicas
    vec_mean = lax.dynamic_slice_in_dim(vec_total, replica_index * shard_len, shard_len, 0)
    vec_new_momentum = momentum_decay * vec_momentum + vec_mean
    vec_new_master = vec_master - step_size * (vec_mean + momentum_decay * vec_new_momentum)
    vec_weights = (vec_base - gain * vec_total).astype(jnp.bfloat16)
    return (
        new_error,
        new_momentum,
        new_master,
        new_weights,
        vec_new_momentum,
        vec_new_master,
        vec_weights,
    )


def solution(mesh):
    grid = Mesh(mesh.devices.reshape(tuple(SIZES.values())), tuple(SIZES))
    dp = ("y", "z", "x")
    return jax.shard_map(
        on_device,
        mesh=grid,
        in_specs=(
            P(dp, None, "c"),
            P(dp, None, "c"),
            P("c", None),
            P(),
            P(dp, "c"),
            P(dp, "c"),
            P(dp, None),
            P(dp),
            P(dp),
        ),
        out_specs=(
            P(dp, None, "c"),
            P(dp, "c"),
            P(dp, "c"),
            P(None, "c"),
            P(dp),
            P(dp),
            P(),
        ),
        check_vma=False,
    )
```

time: 1860 us -> 147 us (0.08)
  blocking collectives: 1360 us -> 22.1 us
  waiting for transfers between devices: 455 us -> 41.5 us
  starting transfers between devices: 0.12 us -> 33.3 us
    unnamed x1 -> x0, blocking collectives: 682 us -> none
    psum x1 -> x0, blocking collectives: 677 us -> none  [on_device(): vec_total = lax.psum(vec_term, 'dp')]
    psum x2 -> x0, waiting for transfers between devices: 455 us -> none  [the longest x1 245 us: on_device(): row_total = lax.psum(row_part, ('dp', 'tensor'))]
    ppermute x0 -> x18, waiting for transfers between devices: none -> 31.9 us  [the longest x17 31 us: exchange(): lax.ppermute(value, axis, [(i, i ^ d) for i in range(n)])]
    ppermute x0 -> x18, starting transfers between devices: none -> 27.9 us  [the longest x17 27.8 us: exchange(): lax.ppermute(value, axis, [(i, i ^ d) for i in range(n)])]
    all_to_all x0 -> x1, blocking collectives: none -> 22.1 us  [on_device(): pieces = lax.all_to_all(pieces, ('z', 'x'), 0, 0, tiled=True)]
  transfers between devices with their start and end apart: 3 -> 20, of which waited for: 2 -> 15; matrix products, arithmetic and copies ran while one was open for 0% -> 10% of each run, Pallas kernels for 0% -> 0%
where the time goes in v1:
time: 147 us; the launch traced here: 146 us
  waiting for transfers between devices  41.5 us (28%)
  starting transfers between devices  33.3 us (23%)
  blocking collectives  22.1 us (15%)
  local copies, waits for them, and re-layouts  14.9 us (10%)
  between operations  14.4 us (10%)
  matrix products  13.7 us (9%)
  other arithmetic  6.32 us (4%)
    ppermute x17, waiting for transfers between devices, exchange(): lax.ppermute(value, axis, [(i, i ^ d) for i in range(n)])  31 us
    ppermute x17, starting transfers between devices, exchange(): lax.ppermute(value, axis, [(i, i ^ d) for i in range(n)])  27.8 us
    all_to_all x1, blocking collectives, on_device(): pieces = lax.all_to_all(pieces, ('z', 'x'), 0, 0, tiled=True)  22.1 us
    all_to_all x1, waiting for transfers between devices, on_device(): pieces = lax.all_to_all(pieces, ('z', 'x'), 0, 0, tiled=True)  9.57 us
    reshape x2, local copies, waits for them, and re-layouts, on_device(): base_all.reshape(nz, ny, -1, cols).swapaxes(0, 1).reshape(width, cols)  8.65 us
    dot_general x1, matrix products, on_device(): lax.dot_general(row_basis, col_mean, (((0,), (0,)), ((), ())), precision=...  6.74 us
    all_to_all x1, starting transfers between devices, on_device(): pieces = lax.all_to_all(pieces, ('z', 'x'), 0, 0, tiled=True)  5.34 us
    dot_general x2, local copies, waits for them, and re-layouts, on_device(): col_part = jnp.dot(basis_b, merged, preferred_element_type=jnp.float32)  4.43 us
  transfers between devices with their start and end apart: 20, of which 15 were waited for; matrix products, arithmetic and copies ran while one was open for 10% of the time, Pallas kernels for 0%

profile of v1, /device:TPU:32, one launch (start us, length us, event | category | flops | bytes accessed | tf_op | source)
XLA Modules:
  0.0 146.2 jit_solution(3261529450420936744)
XLA Ops:
  7.2 0.0 copy-start
  7.2 0.0 all-gather.3.cloned.1.call-start
  7.2 0.0 copy-start.4
  7.3 3.2 %fusion.2 = f32[768,32]{0,1:T(8,128)S(1)} fusion(f32[1536,32]{0,1:T(8,128)} %param.11, bf16[1,768,1536]{2,1,0:T(8,128)(2,1)} %param.10, bf16[1,768,1536]{2,1,0:T(8,128)(2,1)} %param.9), kind=kOutput, calls=%fused_computation.5 | convolution fusion | flops 80265216 | bytes 5013504 | tf_op jit(solution)/shard_map/dot_general | solution.py:50
  10.5 0.1 collective-permute-start
  10.7 0.1 subtract_dynamic-update-slice_fusion
  10.8 0.1 dynamic-slice_bitcast_fusion.1
  11.0 0.9 collective-permute-done
  11.9 2.8 %collective-permute-start.3 = (f32[210,128]{1,0:T(8,128)S(1)}, f32[210,128]{1,0:T(8,128)S(1)}, u32[]{:S(2)}, u32[]{:S(2)}) collective-permute-start(f32[210,128]{1,0:T(8,128)S(1)} %pad_maximum_fusion.2), channel_id=1, source_target_pairs={{0,6},{2,4},{4,2},{6,0},{1,7},{3,5},{5,3},{7,1},{8,14},{10,12},{12... | collective-permute-start | bytes 322568 | tf_op jit(solution)/shard_map/ppermute | solution.py:14
  14.7 0.8 collective-permute-start.2
  15.5 0.5 collective-permute-start.1
  16.1 3.7 %collective-permute-done.3 = f32[210,128]{1,0:T(8,128)S(1)} collective-permute-done((f32[210,128]{1,0:T(8,128)S(1)}, f32[210,128]{1,0:T(8,128)S(1)}, u32[]{:S(2)}, u32[]{:S(2)}) %collective-permute-start.3) | collective-permute-done | bytes 107552 | tf_op jit(solution)/shard_map/ppermute | solution.py:14
  19.8 2.4 %collective-permute-done.2 = f32[210,128]{1,0:T(8,128)S(1)} collective-permute-done((f32[210,128]{1,0:T(8,128)S(1)}, f32[210,128]{1,0:T(8,128)S(1)}, u32[]{:S(2)}, u32[]{:S(2)}) %collective-permute-start.2) | collective-permute-done | bytes 107552 | tf_op jit(solution)/shard_map/ppermute | solution.py:14
  22.2 0.0 collective-permute-done.1
  22.2 0.7 concatenate.28
  22.9 0.0 copy-start.1
  22.9 3.1 %collective-permute-start.6 = (f32[426,128]{1,0:T(8,128)S(1)}, f32[426,128]{1,0:T(8,128)S(1)}, u32[]{:S(2)}, u32[]{:S(2)}) collective-permute-start(f32[426,128]{1,0:T(8,128)S(1)} %concatenate.28), channel_id=1, source_target_pairs={{0,192},{64,128},{128,64},{192,0},{1,193},{65,129},{129,65},{193,1... | collective-permute-start | bytes 654344 | tf_op jit(solution)/shard_map/ppermute | solution.py:14
  26.0 0.6 collective-permute-start.5
  26.7 0.5 collective-permute-start.4
  27.1 6.8 %collective-permute-done.6 = f32[426,128]{1,0:T(8,128)S(1)} collective-permute-done((f32[426,128]{1,0:T(8,128)S(1)}, f32[426,128]{1,0:T(8,128)S(1)}, u32[]{:S(2)}, u32[]{:S(2)}) %collective-permute-start.6) | collective-permute-done | bytes 218144 | tf_op jit(solution)/shard_map/ppermute | solution.py:14
  33.9 1.3 collective-permute-done.5
  35.2 0.1 collective-permute-done.4
  35.3 0.1 broadcast_select_fusion.1
  35.3 0.1 broadcast_select_fusion.3
  35.4 0.9 pad_maximum_fusion
  36.3 0.0 all-gather.3.cloned.1.call-update
  36.3 5.9 %collective-permute-start.13 = (f32[138,128]{1,0:T(8,128)S(1)}, f32[138,128]{1,0:T(8,128)S(1)}, u32[]{:S(2)}, u32[]{:S(2)}) collective-permute-start(f32[138,128]{1,0:T(8,128)S(1)} %fusion.14), channel_id=1, source_target_pairs={{0,56},{8,48},{16,40},{24,32},{32,24},{40,16},{48,8},{56,0},{1,57}... | collective-permute-start | bytes 211976 | tf_op jit(solution)/shard_map/ppermute | solution.py:14
  42.3 0.0 collective-permute-start.12
  42.3 4.6 %collective-permute-start.11 = (f32[138,128]{1,0:T(8,128)S(1)}, f32[138,128]{1,0:T(8,128)S(1)}, u32[]{:S(2)}, u32[]{:S(2)}) collective-permute-start(f32[138,128]{1,0:T(8,128)S(1)} %fusion.14), channel_id=1, source_target_pairs={{0,40},{8,32},{16,56},{24,48},{32,8},{40,0},{48,24},{56,16},{1,41}... | collective-permute-start | bytes 211976 | tf_op jit(solution)/shard_map/ppermute | solution.py:14
  46.8 0.6 collective-permute-start.10
  47.4 1.0 collective-permute-start.9
  48.4 0.0 collective-permute-done.13
  48.4 2.7 %collective-permute-start.8 = (f32[138,128]{1,0:T(8,128)S(1)}, f32[138,128]{1,0:T(8,128)S(1)}, u32[]{:S(2)}, u32[]{:S(2)}) collective-permute-start(f32[138,128]{1,0:T(8,128)S(1)} %fusion.14), channel_id=1, source_target_pairs={{0,16},{8,24},{16,0},{24,8},{32,48},{40,56},{48,32},{56,40},{1,17}... | collective-permute-start | bytes 211976 | tf_op jit(solution)/shard_map/ppermute | solution.py:14
  51.1 0.9 collective-permute-done.12
  52.0 0.0 collective-permute-start.7
  52.0 3.1 %collective-permute-done.11 = f32[138,128]{1,0:T(8,128)S(1)} collective-permute-done((f32[138,128]{1,0:T(8,128)S(1)}, f32[138,128]{1,0:T(8,128)S(1)}, u32[]{:S(2)}, u32[]{:S(2)}) %collective-permute-start.11) | collective-permute-done | bytes 70688 | tf_op jit(solution)/shard_map/ppermute | solution.py:14
  55.1 0.3 collective-permute-done.10
  55.4 5.9 %collective-permute-done.9 = f32[138,128]{1,0:T(8,128)S(1)} collective-permute-done((f32[138,128]{1,0:T(8,128)S(1)}, f32[138,128]{1,0:T(8,128)S(1)}, u32[]{:S(2)}, u32[]{:S(2)}) %collective-permute-start.9) | collective-permute-done | bytes 70688 | tf_op jit(solution)/shard_map/ppermute | solution.py:14
  61.3 0.7 collective-permute-done.8
  62.0 1.7 %collective-permute-done.7 = f32[138,128]{1,0:T(8,128)S(1)} collective-permute-done((f32[138,128]{1,0:T(8,128)S(1)}, f32[138,128]{1,0:T(8,128)S(1)}, u32[]{:S(2)}, u32[]{:S(2)}) %collective-permute-start.7) | collective-permute-done | bytes 70688 | tf_op jit(solution)/shard_map/ppermute | solution.py:14
  63.8 0.1 collective-permute-start.14
  63.9 3.7 %fusion.30 = bf16[1536,768]{0,1:T(8,128)(2,1)} fusion(bf16[1,768,1536]{2,1,0:T(8,128)(2,1)S(1)} %copy-done.1, bf16[1,768,1536]{2,1,0:T(8,128)(2,1)} %param.9), kind=kLoop, calls=%fused_computation.79 | loop fusion | flops 4718592 | bytes 7077888 | tf_op jit(solution)/shard_map/dot_general | solution.py:96
  67.6 4.3 %copy.20 = bf16[1536,768]{1,0:T(8,128)(2,1)} copy(bf16[1536,768]{0,1:T(8,128)(2,1)} %fusion.30) | data formatting | bytes 4718592 | tf_op jit(solution)/shard_map/dot_general | solution.py:96
  71.9 0.0 collective-permute-done.14
  72.0 0.3 fusion.10
  72.3 0.0 copy-start.5
  72.3 2.5 %fusion.16 = f32[32,12,128]{2,0,1:T(8,128)S(1)} fusion(bf16[12,128,768]{2,1,0:T(8,128)(2,1)} %bitcast.47, f32[768,32]{0,1:T(8,128)S(1)} %fusion.10), kind=kOutput, calls=%fused_computation.37 | convolution fusion | flops 75522048 | bytes 2654208 | tf_op jit(solution)/shard_map/dot_general | solution.py:96
  74.8 0.1 copy.21
  74.9 22.1 %all_to_all.10 = f32[32,12,128]{2,1,0:T(8,128)S(1)} all-to-all(f32[32,12,128]{2,1,0:T(8,128)S(1)} %copy.21), channel_id=1, replica_groups=mesh['y'=4,'z'=8,'x'=4,'c'=2] {'z','x'}, dimensions={0} | all-to-all | bytes 393216 | tf_op jit(solution)/shard_map/all_to_all | solution.py:100
  97.1 3.6 %collective-permute-start.17 = (f32[12,128]{1,0:T(8,128)S(1)}, f32[12,128]{1,0:T(8,128)S(1)}, u32[]{:S(2)}, u32[]{:S(2)}) collective-permute-start(f32[12,128]{1,0:T(8,128)S(1)} %reduce_sum.9), channel_id=1, source_target_pairs={{0,192},{64,128},{128,64},{192,0},{1,193},{65,129},{129,65},{193,1... | collective-permute-start | bytes 18440 | tf_op jit(solution)/shard_map/ppermute | solution.py:14
  100.7 1.0 collective-permute-start.15
  101.7 0.7 collective-permute-done.17
  102.3 3.5 %collective-permute-done.16 = f32[12,128]{1,0:T(8,128)S(1)} collective-permute-done((f32[12,128]{1,0:T(8,128)S(1)}, f32[12,128]{1,0:T(8,128)S(1)}, u32[]{:S(2)}, u32[]{:S(2)}) %collective-permute-start.16) | collective-permute-done | bytes 6176 | tf_op jit(solution)/shard_map/ppermute | solution.py:14
  105.9 0.0 collective-permute-done.15
  105.9 0.7 broadcast_in_dim.13
  106.6 5.3 %all-to-all-start.1 = ((f32[32,12,128]{2,1,0:T(8,128)}), f32[32,12,128]{2,1,0:T(8,128)S(1)}, u32[]{:S(2)}, u32[]{:S(2)}) async-start(f32[32,12,128]{2,1,0:T(8,128)} %broadcast_in_dim.13), calls=%async_computation.1 | async-start | bytes 524288 | tf_op jit(solution)/shard_map/all_to_all | solution.py:103
  112.0 0.6 fusion.22
  112.6 0.6 multiply_subtract_fusion.2
  113.2 9.6 %all-to-all-done.1 = f32[32,12,128]{2,1,0:T(8,128)S(1)} async-done(((f32[32,12,128]{2,1,0:T(8,128)}), f32[32,12,128]{2,1,0:T(8,128)S(1)}, u32[]{:S(2)}, u32[]{:S(2)}) %all-to-all-start.1) | async-done | bytes 196640 | tf_op jit(solution)/shard_map/all_to_all | solution.py:103
  122.8 1.0 multiply_subtract_fusion
  123.8 5.8 %reshape.69 = f32[8,4,24,1536]{3,2,1,0:T(8,128)} reshape(f32[9216,128]{1,0:T(8,128)} %all-gather.3.cloned.1.call-done) | data formatting | bytes 9437184 | tf_op jit(solution)/shard_map/reshape | solution.py:112
  129.5 2.9 %copy.22 = f32[8,4,24,1536]{3,2,0,1:T(8,128)S(1)} copy(f32[8,4,24,1536]{3,2,1,0:T(8,128)} %reshape.69) | data formatting | bytes 9437184 | tf_op jit(solution)/shard_map/reshape | solution.py:112
  132.4 0.2 copy-done.2
  132.6 6.7 %fusion = (bf16[768,1536]{1,0:T(8,128)(2,1)}, bf16[1,768,1536]{2,1,0:T(8,128)(2,1)}) fusion(f32[8,4,24,1536]{3,2,0,1:T(8,128)S(1)} %copy.22, bf16[1,768,1536]{2,1,0:T(8,128)(2,1)S(1)} %copy-done.1, bf16[1,768,1536]{2,1,0:T(8,128)(2,1)S(1)} %copy-done.2, f32[768,32]{0,1:T(8,128)S(1)} %fusion.10, f32[4,8,12,128]{3,2,1,0:T(8,128)S(1)} %bitcast.49), kind=kOutput, calls=%fused_computation.1 | convolution fusion | flops 464781312 | bytes 14450688 | tf_op jit(solution)/shard_map/dot_general | solution.py:106
  (36 shorter events, 0.4 us)
Async XLA Ops:
  7.2 64.8 %copy-start = (f32[32,32]{1,0:T(8,128)S(1)}, f32[32,32]{1,0:T(8,128)}, u32[]{:S(2)}) copy-start(f32[32,32]{1,0:T(8,128)} %param.12) | copy-start | bytes 12292
  7.2 116.6 %all-gather.3.cloned.1.call-start = ((), (), s32[]{:S(2)}) async-start(), calls=%async_computation.2 | async-start | bytes 5308416 | tf_op jit(solution)/shard_map/all_gather | solution.py:80
  7.2 3.4 %copy-start.3 = (f32[6,1536]{1,0:T(8,128)S(1)}, f32[6,1536]{1,0:T(8,128)}, u32[]{:S(2)}) copy-start(f32[6,1536]{1,0:T(8,128)} %param.13) | copy-start | bytes 110596
  7.2 3.4 %copy-start.4 = (f32[6,1536]{1,0:T(8,128)S(1)}, f32[6,1536]{1,0:T(8,128)}, u32[]{:S(2)}) copy-start(f32[6,1536]{1,0:T(8,128)} %param.14) | copy-start | bytes 110596
  7.3 3.4 %copy-start.7 = (f32[42]{0:T(128)S(1)}, f32[42]{0:T(128)}, u32[]{:S(2)}) copy-start(f32[42]{0:T(128)} %param.16) | copy-start | bytes 508
  7.3 3.4 %copy-start.8 = (f32[42]{0:T(128)S(1)}, f32[42]{0:T(128)}, u32[]{:S(2)}) copy-start(f32[42]{0:T(128)} %param.17) | copy-start | bytes 508
  7.3 3.6 %copy-start.6 = (bf16[1,5376]{1,0:T(2,128)(2,1)S(1)}, bf16[1,5376]{1,0:T(2,128)(2,1)}, u32[]{:S(2)}) copy-start(bf16[1,5376]{1,0:T(2,128)(2,1)} %param.15) | copy-start | bytes 32260
  10.5 1.3 collective-permute-start
  11.9 7.9 %collective-permute-start.3 = (f32[210,128]{1,0:T(8,128)S(1)}, f32[210,128]{1,0:T(8,128)S(1)}, u32[]{:S(2)}, u32[]{:S(2)}) collective-permute-start(f32[210,128]{1,0:T(8,128)S(1)} %pad_maximum_fusion.2), channel_id=1, source_target_pairs={{0,6},{2,4},{4,2},{6,0},{1,7},{3,5},{5,3},{7,1},{8,14},{10,12},{12... | collective-permute-start | bytes 322568 | tf_op jit(solution)/shard_map/ppermute | solution.py:14
  14.7 7.4 %collective-permute-start.2 = (f32[210,128]{1,0:T(8,128)S(1)}, f32[210,128]{1,0:T(8,128)S(1)}, u32[]{:S(2)}, u32[]{:S(2)}) collective-permute-start(f32[210,128]{1,0:T(8,128)S(1)} %pad_maximum_fusion.2), channel_id=1, source_target_pairs={{0,4},{2,6},{4,0},{6,2},{1,5},{3,7},{5,1},{7,3},{8,12},{10,14},{12... | collective-permute-start | bytes 322568 | tf_op jit(solution)/shard_map/ppermute | solution.py:14
  15.5 6.7 %collective-permute-start.1 = (f32[210,128]{1,0:T(8,128)S(1)}, f32[210,128]{1,0:T(8,128)S(1)}, u32[]{:S(2)}, u32[]{:S(2)}) collective-permute-start(f32[210,128]{1,0:T(8,128)S(1)} %pad_maximum_fusion.2), channel_id=1, source_target_pairs={{0,2},{2,0},{4,6},{6,4},{1,3},{3,1},{5,7},{7,5},{8,10},{10,8},{12,... | collective-permute-start | bytes 322568 | tf_op jit(solution)/shard_map/ppermute | solution.py:14
  22.9 41.0 %copy-start.1 = (bf16[1,768,1536]{2,1,0:T(8,128)(2,1)S(1)}, bf16[1,768,1536]{2,1,0:T(8,128)(2,1)}, u32[]{:S(2)}) copy-start(bf16[1,768,1536]{2,1,0:T(8,128)(2,1)} %param.10) | copy-start | bytes 7077892
  22.9 11.0 %collective-permute-start.6 = (f32[426,128]{1,0:T(8,128)S(1)}, f32[426,128]{1,0:T(8,128)S(1)}, u32[]{:S(2)}, u32[]{:S(2)}) collective-permute-start(f32[426,128]{1,0:T(8,128)S(1)} %concatenate.28), channel_id=1, source_target_pairs={{0,192},{64,128},{128,64},{192,0},{1,193},{65,129},{129,65},{193,1... | collective-permute-start | bytes 654344 | tf_op jit(solution)/shard_map/ppermute | solution.py:14
  26.0 9.1 %collective-permute-start.5 = (f32[426,128]{1,0:T(8,128)S(1)}, f32[426,128]{1,0:T(8,128)S(1)}, u32[]{:S(2)}, u32[]{:S(2)}) collective-permute-start(f32[426,128]{1,0:T(8,128)S(1)} %concatenate.28), channel_id=1, source_target_pairs={{0,128},{64,192},{128,0},{192,64},{1,129},{65,193},{129,1},{193,65... | collective-permute-start | bytes 654344 | tf_op jit(solution)/shard_map/ppermute | solution.py:14
  26.7 8.6 %collective-permute-start.4 = (f32[426,128]{1,0:T(8,128)S(1)}, f32[426,128]{1,0:T(8,128)S(1)}, u32[]{:S(2)}, u32[]{:S(2)}) collective-permute-start(f32[426,128]{1,0:T(8,128)S(1)} %concatenate.28), channel_id=1, source_target_pairs={{0,64},{64,0},{128,192},{192,128},{1,65},{65,1},{129,193},{193,129... | collective-permute-start | bytes 654344 | tf_op jit(solution)/shard_map/ppermute | solution.py:14
  36.3 12.1 %collective-permute-start.13 = (f32[138,128]{1,0:T(8,128)S(1)}, f32[138,128]{1,0:T(8,128)S(1)}, u32[]{:S(2)}, u32[]{:S(2)}) collective-permute-start(f32[138,128]{1,0:T(8,128)S(1)} %fusion.14), channel_id=1, source_target_pairs={{0,56},{8,48},{16,40},{24,32},{32,24},{40,16},{48,8},{56,0},{1,57}... | collective-permute-start | bytes 211976 | tf_op jit(solution)/shard_map/ppermute | solution.py:14
  42.3 9.8 %collective-permute-start.12 = (f32[138,128]{1,0:T(8,128)S(1)}, f32[138,128]{1,0:T(8,128)S(1)}, u32[]{:S(2)}, u32[]{:S(2)}) collective-permute-start(f32[138,128]{1,0:T(8,128)S(1)} %fusion.14), channel_id=1, source_target_pairs={{0,48},{8,56},{16,32},{24,40},{32,16},{40,24},{48,0},{56,8},{1,49}... | collective-permute-start | bytes 211976 | tf_op jit(solution)/shard_map/ppermute | solution.py:14
  42.3 12.9 %collective-permute-start.11 = (f32[138,128]{1,0:T(8,128)S(1)}, f32[138,128]{1,0:T(8,128)S(1)}, u32[]{:S(2)}, u32[]{:S(2)}) collective-permute-start(f32[138,128]{1,0:T(8,128)S(1)} %fusion.14), channel_id=1, source_target_pairs={{0,40},{8,32},{16,56},{24,48},{32,8},{40,0},{48,24},{56,16},{1,41}... | collective-permute-start | bytes 211976 | tf_op jit(solution)/shard_map/ppermute | solution.py:14
  46.8 8.6 %collective-permute-start.10 = (f32[138,128]{1,0:T(8,128)S(1)}, f32[138,128]{1,0:T(8,128)S(1)}, u32[]{:S(2)}, u32[]{:S(2)}) collective-permute-start(f32[138,128]{1,0:T(8,128)S(1)} %fusion.14), channel_id=1, source_target_pairs={{0,32},{8,40},{16,48},{24,56},{32,0},{40,8},{48,16},{56,24},{1,33}... | collective-permute-start | bytes 211976 | tf_op jit(solution)/shard_map/ppermute | solution.py:14
  47.4 13.9 %collective-permute-start.9 = (f32[138,128]{1,0:T(8,128)S(1)}, f32[138,128]{1,0:T(8,128)S(1)}, u32[]{:S(2)}, u32[]{:S(2)}) collective-permute-start(f32[138,128]{1,0:T(8,128)S(1)} %fusion.14), channel_id=1, source_target_pairs={{0,24},{8,16},{16,8},{24,0},{32,56},{40,48},{48,40},{56,32},{1,25}... | collective-permute-start | bytes 211976 | tf_op jit(solution)/shard_map/ppermute | solution.py:14
  48.4 13.6 %collective-permute-start.8 = (f32[138,128]{1,0:T(8,128)S(1)}, f32[138,128]{1,0:T(8,128)S(1)}, u32[]{:S(2)}, u32[]{:S(2)}) collective-permute-start(f32[138,128]{1,0:T(8,128)S(1)} %fusion.14), channel_id=1, source_target_pairs={{0,16},{8,24},{16,0},{24,8},{32,48},{40,56},{48,32},{56,40},{1,17}... | collective-permute-start | bytes 211976 | tf_op jit(solution)/shard_map/ppermute | solution.py:14
  52.0 11.7 %collective-permute-start.7 = (f32[138,128]{1,0:T(8,128)S(1)}, f32[138,128]{1,0:T(8,128)S(1)}, u32[]{:S(2)}, u32[]{:S(2)}) collective-permute-start(f32[138,128]{1,0:T(8,128)S(1)} %fusion.14), channel_id=1, source_target_pairs={{0,8},{8,0},{16,24},{24,16},{32,40},{40,32},{48,56},{56,48},{1,9},... | collective-permute-start | bytes 211976 | tf_op jit(solution)/shard_map/ppermute | solution.py:14
  63.8 8.1 %collective-permute-start.14 = (f32[138,128]{1,0:T(8,128)S(1)}, f32[138,128]{1,0:T(8,128)S(1)}, u32[]{:S(2)}, u32[]{:S(2)}) collective-permute-start(f32[138,128]{1,0:T(8,128)S(1)} %add_add_fusion), channel_id=1, source_target_pairs={{0,1},{1,0},{2,3},{3,2},{4,5},{5,4},{6,7},{7,6},{8,9},{9,8},{10,11... | collective-permute-start | bytes 211976 | tf_op jit(solution)/shard_map/ppermute | solution.py:14
  72.3 50.5 %copy-start.5 = (f32[6,1536]{1,0:T(8,128)S(1)}, f32[6,1536]{1,0:T(8,128)}, u32[]{:S(2)}) copy-start(f32[6,1536]{1,0:T(8,128)} %param.14) | copy-start | bytes 110596
  97.1 5.2 %collective-permute-start.17 = (f32[12,128]{1,0:T(8,128)S(1)}, f32[12,128]{1,0:T(8,128)S(1)}, u32[]{:S(2)}, u32[]{:S(2)}) collective-permute-start(f32[12,128]{1,0:T(8,128)S(1)} %reduce_sum.9), channel_id=1, source_target_pairs={{0,192},{64,128},{128,64},{192,0},{1,193},{65,129},{129,65},{193,1... | collective-permute-start | bytes 18440 | tf_op jit(solution)/shard_map/ppermute | solution.py:14
  100.7 5.2 %collective-permute-start.16 = (f32[12,128]{1,0:T(8,128)S(1)}, f32[12,128]{1,0:T(8,128)S(1)}, u32[]{:S(2)}, u32[]{:S(2)}) collective-permute-start(f32[12,128]{1,0:T(8,128)S(1)} %reduce_sum.9), channel_id=1, source_target_pairs={{0,128},{64,192},{128,0},{192,64},{1,129},{65,193},{129,1},{193,65... | collective-permute-start | bytes 18440 | tf_op jit(solution)/shard_map/ppermute | solution.py:14
  100.7 5.2 %collective-permute-start.15 = (f32[12,128]{1,0:T(8,128)S(1)}, f32[12,128]{1,0:T(8,128)S(1)}, u32[]{:S(2)}, u32[]{:S(2)}) collective-permute-start(f32[12,128]{1,0:T(8,128)S(1)} %reduce_sum.9), channel_id=1, source_target_pairs={{0,64},{64,0},{128,192},{192,128},{1,65},{65,1},{129,193},{193,129... | collective-permute-start | bytes 18440 | tf_op jit(solution)/shard_map/ppermute | solution.py:14
  106.6 16.2 %all-to-all-start.1 = ((f32[32,12,128]{2,1,0:T(8,128)}), f32[32,12,128]{2,1,0:T(8,128)S(1)}, u32[]{:S(2)}, u32[]{:S(2)}) async-start(f32[32,12,128]{2,1,0:T(8,128)} %broadcast_in_dim.13), calls=%async_computation.1 | async-start | bytes 524288 | tf_op jit(solution)/shard_map/all_to_all | solution.py:103
  129.5 3.1 %copy-start.2 = (bf16[1,768,1536]{2,1,0:T(8,128)(2,1)S(1)}, bf16[1,768,1536]{2,1,0:T(8,128)(2,1)}, u32[]{:S(2)}) copy-start(bf16[1,768,1536]{2,1,0:T(8,128)(2,1)} %param.9) | copy-start | bytes 7077892
Sparse Core Ops, SparseCore 0:
  36.4 73.1 all-gather.2

commit v2 on v0

v2 whole, which is shorter than its diff:
```python
import functools

import jax
import jax.numpy as jnp
from jax import lax
from jax.experimental import pallas as pl
from jax.experimental.pallas import tpu as pltpu
from jax.sharding import Mesh, PartitionSpec as P

momentum_decay = 0.9
step_size = 0.5
gain = step_size * (1.0 + momentum_decay)
carried = step_size * momentum_decay * momentum_decay
SIZES = {"y": 4, "z": 8, "x": 4, "c": 2}
REPLICAS = SIZES["y"] * SIZES["z"] * SIZES["x"]
LANES = 128
VMEM = 20 << 20


def flips(value, axis, among=None):
    n = SIZES[axis]
    return [
        lax.ppermute(value, axis, [(i, i ^ d) for i in range(n)]) if d else value
        for d in among or range(n)
    ]


def total(blocks):
    while len(blocks) > 1:
        blocks = [blocks[j] + blocks[j + 1] for j in range(0, len(blocks), 2)]
    return blocks[0]


def merge(grads, error):
    return (grads.astype(jnp.float32) + error.astype(jnp.float32)).astype(jnp.bfloat16)


HBM = pl.BlockSpec(memory_space=pltpu.HBM)


def row_kernel(
    query_hbm, grads_hbm, error_hbm, master_hbm, momentum_hbm, merged_ref, payload_ref, other_ref,
    query, grads, error, master, momentum, sems,
):
    n_blocks = grads_hbm.shape[0] // LANES
    copies = [pltpu.make_async_copy(query_hbm, query, sems.at[0])]
    for i in range(n_blocks):
        at = pl.ds(i * LANES, LANES)
        copies.append(pltpu.make_async_copy(grads_hbm.at[at], grads.at[at], sems.at[1 + 2 * i]))
        copies.append(pltpu.make_async_copy(error_hbm.at[at], error.at[at], sems.at[2 + 2 * i]))
    copies.append(pltpu.make_async_copy(master_hbm, master, sems.at[1 + 2 * n_blocks]))
    copies.append(pltpu.make_async_copy(momentum_hbm, momentum, sems.at[2 + 2 * n_blocks]))
    for copy in copies:
        copy.start()
    copies[0].wait()
    query_b = query[...].astype(jnp.bfloat16)
    first = lax.axis_index("c") == 0
    half = query_b.shape[0] // 2
    for i in range(n_blocks):
        at = pl.ds(i * LANES, LANES)
        copies[1 + 2 * i].wait()
        copies[2 + 2 * i].wait()
        merged = merge(grads[at, :], error[at, :])
        merged_ref[at, :] = merged
        part = lax.dot_general(
            query_b, merged, (((1,), (1,)), ((), ())), preferred_element_type=jnp.float32
        )
        low, high = part[:half], part[half:]
        payload_ref[i * half : (i + 1) * half, :] = jnp.where(first, low, high)
        other_ref[i * half : (i + 1) * half, :] = jnp.where(first, high, low)
    copies[-2].wait()
    copies[-1].wait()
    base = master[...] - carried * momentum[...]
    groups = base.shape[1] // LANES
    n_sums = other_ref.shape[0]
    for r in range(base.shape[0]):
        for g in range(groups):
            row = n_sums + r * groups + g
            payload_ref[row : row + 1, :] = base[r : r + 1, g * LANES : (g + 1) * LANES]


def row_call(query_t, grads, error, master, momentum):
    rank, cols = query_t.shape
    rows = grads.shape[0]
    n_sums = rank // 2 * rows // LANES
    n_base = master.size // LANES
    return pl.pallas_call(
        row_kernel,
        in_specs=[HBM] * 5,
        out_shape=[
            jax.ShapeDtypeStruct(grads.shape, jnp.bfloat16),
            jax.ShapeDtypeStruct((n_sums + n_base, LANES), jnp.float32),
            jax.ShapeDtypeStruct((n_sums, LANES), jnp.float32),
        ],
        scratch_shapes=[
            pltpu.VMEM(query_t.shape, jnp.float32),
            pltpu.VMEM(grads.shape, jnp.bfloat16),
            pltpu.VMEM(grads.shape, jnp.bfloat16),
            pltpu.VMEM(master.shape, jnp.float32),
            pltpu.VMEM(master.shape, jnp.float32),
            pltpu.SemaphoreType.DMA((3 + 2 * (rows // LANES),)),
        ],
        compiler_params=pltpu.CompilerParams(vmem_limit_bytes=VMEM),
        name="row_sum",
    )(query_t, grads, error, master, momentum)


def pair_kernel(n_sums, own_ref, other_ref, out_ref):
    n = own_ref.shape[0] - n_sums
    out_ref[:n_sums, :] = own_ref[:n_sums, :] + other_ref[:n_sums, :]
    out_ref[n_sums : n_sums + n, :] = own_ref[n_sums:, :]
    out_ref[n_sums + n :, :] = other_ref[n_sums:, :]


def spread_kernel(n_sums, *refs):
    *blocks, out_ref = refs
    for k, term in enumerate(thirds(total([b[:n_sums, :] for b in blocks]))):
        out_ref[k * n_sums : (k + 1) * n_sums, :] = term
    n = blocks[0].shape[0] - n_sums
    for j, b in enumerate(blocks):
        first = 3 * n_sums + j * n
        out_ref[first : first + n, :] = b[n_sums:, :].astype(jnp.bfloat16)


def collect_kernel(n_sums, *refs):
    *blocks, sums_ref, base_ref = refs
    term = lambda b, k: b[k * n_sums : (k + 1) * n_sums, :].astype(jnp.float32)
    sums_ref[...] = total([term(b, 0) + (term(b, 1) + term(b, 2)) for b in blocks])
    n = blocks[0].shape[0] - 3 * n_sums
    for j, b in enumerate(blocks):
        base_ref[j * n : (j + 1) * n, :] = b[3 * n_sums :, :]


def blocks_call(kernel, blocks, n_sums, out_shape):
    return pl.pallas_call(
        functools.partial(kernel, n_sums),
        out_shape=out_shape,
        compiler_params=pltpu.CompilerParams(vmem_limit_bytes=VMEM),
        name=kernel.__name__,
    )(*blocks)


def column_kernel(own_ref, other_ref, gram_ref, merged_ref, vec_ref, basis_ref, piece_ref, basis_b):
    step = pl.program_id(0)
    groups = merged_ref.shape[1] // LANES
    half = own_ref.shape[0] // (basis_b.shape[1] // LANES)

    @pl.when(step == 0)
    def _():
        first = lax.axis_index("c") == 0
        own, other = own_ref[...], other_ref[...]
        low, high = jnp.where(first, own, other), jnp.where(first, other, own)
        rows = [
            jnp.concatenate([low[g * half : (g + 1) * half], high[g * half : (g + 1) * half]], 0)
            for g in range(basis_b.shape[1] // LANES)
        ]
        basis = lax.dot_general(
            gram_ref[...],
            jnp.concatenate(rows, 1) / REPLICAS,
            (((0,), (0,)), ((), ())),
            precision=lax.Precision.HIGHEST,
            preferred_element_type=jnp.float32,
        )
        width = basis_ref.shape[2]
        for k in range(basis_ref.shape[0]):
            basis_ref[k] = basis[:, k * width : (k + 1) * width]
        basis_b[...] = basis.astype(jnp.bfloat16)
        n_vec = vec_ref.shape[1]
        piece_ref[:, piece_ref.shape[1] - n_vec :, :] = vec_ref[...]

    part = jnp.dot(basis_b[...], merged_ref[...], preferred_element_type=jnp.float32)
    for j in range(pl.cdiv(piece_ref.shape[1] - vec_ref.shape[1], groups)):

        @pl.when(step == j)
        def _():
            for g in range(groups):
                piece_ref[:, j * groups + g, :] = part[:, g * LANES : (g + 1) * LANES]


def column_call(own, other, gram_inverse, merged, vec):
    rank = gram_inverse.shape[0]
    rows, cols = merged.shape
    block = 512
    pieces = cols // LANES + vec.shape[1]
    basis_shape = (SIZES["y"], rank, rows // SIZES["y"])
    whole = lambda *shape: pl.BlockSpec(shape, lambda j: (0,) * len(shape))
    return pl.pallas_call(
        column_kernel,
        grid=(cols // block,),
        in_specs=[
            whole(*own.shape),
            whole(*own.shape),
            whole(rank, rank),
            pl.BlockSpec((rows, block), lambda j: (0, j)),
            whole(*vec.shape),
        ],
        out_specs=[whole(*basis_shape), whole(rank, pieces, LANES)],
        scratch_shapes=[pltpu.VMEM((rank, rows), jnp.bfloat16)],
        out_shape=[
            jax.ShapeDtypeStruct(basis_shape, jnp.float32),
            jax.ShapeDtypeStruct((rank, pieces, LANES), jnp.float32),
        ],
        compiler_params=pltpu.CompilerParams(vmem_limit_bytes=VMEM),
        name="column_sum",
    )(own, other, gram_inverse, merged, vec)


def thirds(value):
    high = value.astype(jnp.bfloat16)
    rest = value - high.astype(jnp.float32)
    middle = rest.astype(jnp.bfloat16)
    return high, middle, (rest - middle.astype(jnp.float32)).astype(jnp.bfloat16)


def product(rows, cols3):
    high, middle, low = thirds(rows)
    left = jnp.concatenate([high, high, middle, high, low, middle], 0)
    return lax.dot_general(left, cols3, (((0,), (0,)), ((), ())), preferred_element_type=jnp.float32)


def apply_kernel(
    where, own_basis_ref, piece_ref, merged_ref, basis_hbm, base0, base1, base2, base3, master_hbm, momentum_hbm,
    new_error_ref, weights_ref, new_master_ref, new_momentum_ref,
    cols3, lane_rows, basis, base_blocks, master, momentum, sems,
):
    step = pl.program_id(0)
    cols = merged_ref.shape[1]
    groups = cols // LANES
    nx, ny, nz = SIZES["x"], SIZES["y"], SIZES["z"]
    shard = base0.shape[0] // (nx * nz)
    sources = (basis_hbm, base0, base1, base2, base3, master_hbm, momentum_hbm)
    targets = (basis, *[base_blocks.at[k] for k in range(ny)], master, momentum)
    copies = [pltpu.make_async_copy(s, t, sems.at[k]) for k, (s, t) in enumerate(zip(sources, targets))]

    @pl.when(step == 0)
    def _():
        for copy in copies:
            copy.start()
        col = jnp.concatenate([piece_ref[:, g, :] for g in range(groups)], 1) / REPLICAS
        high, middle, low = thirds(col)
        cols3[...] = jnp.concatenate([high, middle, high, low, high, middle], 0)
        copies[0].wait()

    for k in range(ny):

        @pl.when(step == k)
        def _():
            copies[1 + k].wait()
            for j in range(nx):
                for d in range(nz):
                    place = (where[1] ^ (d // 2) ^ (d % 2 * 6)) * nx + (where[2] ^ j)
                    source = (j * nz + d) * shard
                    lane_rows[pl.ds(pl.multiple_of(place * shard, 8), shard), :] = base_blocks[
                        k, source : source + shard, :
                    ].astype(jnp.float32)

    approx = product(basis[where[0] ^ step], cols3[...])
    new_error_ref[...] = (merged_ref[...].astype(jnp.float32) - approx).astype(jnp.bfloat16)
    for g in range(groups):
        lanes = slice(g * LANES, (g + 1) * LANES)
        value = lane_rows[pl.ds(g, merged_ref.shape[0], stride=groups), :]
        weights_ref[:, lanes] = (value - gain * approx[:, lanes]).astype(jnp.bfloat16)

    @pl.when(step == ny - 1)
    def _():
        copies[-2].wait()
        copies[-1].wait()
        rows_approx = product(own_basis_ref[...], cols3[...])
        new = momentum_decay * momentum[...] + rows_approx
        new_momentum_ref[...] = new
        new_master_ref[...] = master[...] - step_size * (rows_approx + momentum_decay * new)


def apply_call(where, row_basis, own_basis, pieces, merged, bases, master, momentum):
    _, rank, block = row_basis.shape
    rows, cols = merged.shape
    spec = pl.BlockSpec((block, cols), lambda i, s: (s[0] ^ i, 0))
    whole = lambda v: pl.BlockSpec(v.shape, lambda i, s: (0,) * v.ndim)
    return pl.pallas_call(
        apply_kernel,
        grid_spec=pltpu.PrefetchScalarGridSpec(
            num_scalar_prefetch=1,
            grid=(SIZES["y"],),
            in_specs=[whole(own_basis), whole(pieces), spec, *[HBM] * (3 + len(bases))],
            out_specs=[spec, spec, whole(master), whole(momentum)],
            scratch_shapes=[
                pltpu.VMEM((6 * rank, cols), jnp.bfloat16),
                pltpu.VMEM(bases[0].shape, jnp.float32),
                pltpu.VMEM(row_basis.shape, jnp.float32),
                pltpu.VMEM((len(bases), *bases[0].shape), jnp.bfloat16),
                pltpu.VMEM(master.shape, jnp.float32),
                pltpu.VMEM(master.shape, jnp.float32),
                pltpu.SemaphoreType.DMA((3 + len(bases),)),
            ],
        ),
        out_shape=[
            jax.ShapeDtypeStruct((rows, cols), jnp.bfloat16),
            jax.ShapeDtypeStruct((rows, cols), jnp.bfloat16),
            jax.ShapeDtypeStruct(master.shape, jnp.float32),
            jax.ShapeDtypeStruct(master.shape, jnp.float32),
        ],
        compiler_params=pltpu.CompilerParams(vmem_limit_bytes=VMEM),
        name="apply",
    )(where, own_basis, pieces, merged, row_basis, *bases, master, momentum)


def vec_rows_of(rank, replica_index, vec_grads, vec_master, vec_momentum):
    vec_base = lax.dynamic_update_slice_in_dim(
        jnp.zeros((vec_grads.shape[1],), jnp.float32),
        vec_master - carried * vec_momentum,
        replica_index * vec_master.shape[0],
        0,
    )
    vec = jnp.concatenate([vec_grads[0].astype(jnp.float32), vec_base], 0)
    vec_rows = pl.cdiv(vec.shape[0], rank * LANES)
    vec = jnp.pad(vec, (0, vec_rows * rank * LANES - vec.shape[0]))
    return vec.reshape(rank, vec_rows, LANES)


def on_device(
    fc_grads,
    fc_error,
    query,
    gram_inverse,
    fc_master,
    fc_momentum,
    vec_grads,
    vec_master,
    vec_momentum,
):
    x, y, z, c = (lax.axis_index(a) for a in "xyzc")
    replica_index = (y * SIZES["z"] + z) * SIZES["x"] + x
    grads, error = fc_grads[0], fc_error[0]
    rank = query.shape[1]

    merged, payload, row_other = row_call(query.T, grads, error, fc_master, fc_momentum)
    n_sums = row_other.shape[0]
    row_other = lax.ppermute(row_other, "c", [(0, 1), (1, 0)])
    payload = payload + jnp.pad(row_other, ((0, payload.shape[0] - n_sums), (0, 0)))
    n_base = payload.shape[0] - n_sums
    lanes = lambda rows, dtype: jax.ShapeDtypeStruct((rows, LANES), dtype)
    payload = blocks_call(
        pair_kernel, flips(payload, "z", (0, 6)), n_sums, lanes(n_sums + 2 * n_base, jnp.float32)
    )
    payload = blocks_call(
        spread_kernel,
        flips(payload, "z", (0, 1, 2, 3)),
        n_sums,
        lanes(3 * n_sums + 8 * n_base, jnp.bfloat16),
    )
    sums, base = blocks_call(
        collect_kernel,
        flips(payload, "x"),
        n_sums,
        [lanes(n_sums, jnp.float32), lanes(32 * n_base, jnp.bfloat16)],
    )
    vec = vec_rows_of(rank, replica_index, vec_grads, vec_master, vec_momentum)
    sums, vec = lax.optimization_barrier((sums, vec))
    sums = total(flips(sums, "y"))
    bases = flips(base, "y")
    own, other = flips(sums, "c")
    own, other, bases[0] = lax.optimization_barrier((own, other, bases[0]))

    vec_len = vec_grads.shape[1]
    shard_len = vec_master.shape[0]
    vec_rows = vec.shape[1]
    row_basis, pieces = column_call(own, other, gram_inverse, merged, vec)
    state_rows = fc_master.shape[0]
    own_basis = lax.dynamic_slice(
        row_basis, (y, 0, (z * SIZES["x"] + x) * state_rows), (1, rank, state_rows)
    )[0]

    pieces = lax.all_to_all(pieces, ("z", "x"), 0, 0, tiled=True)
    piece = total(flips(jnp.sum(pieces, 0), "y"))
    piece, *bases = lax.optimization_barrier((piece, *bases))
    pieces = jnp.broadcast_to(piece[None], (rank,) + piece.shape)
    pieces = lax.all_to_all(pieces, ("z", "x"), 0, 0, tiled=True)

    where = jnp.stack([y, z, x]).astype(jnp.int32)
    new_error, new_weights, new_master, new_momentum = apply_call(
        where, row_basis, own_basis, pieces, merged, bases, fc_master, fc_momentum
    )

    vec = pieces[:, -vec_rows:].reshape(-1)
    vec_total = vec[:vec_len] / REPLICAS
    vec_base = vec[vec_len : 2 * vec_len]
    vec_mean = lax.dynamic_slice_in_dim(vec_total, replica_index * shard_len, shard_len, 0)
    vec_new_momentum = momentum_decay * vec_momentum + vec_mean
    vec_new_master = vec_master - step_size * (vec_mean + momentum_decay * vec_new_momentum)
    vec_weights = (vec_base - gain * vec_total).astype(jnp.bfloat16)
    return (
        new_error[None],
        new_momentum,
        new_master,
        new_weights,
        vec_new_momentum,
        vec_new_master,
        vec_weights,
    )


def solution(mesh):
    grid = Mesh(mesh.devices.reshape(tuple(SIZES.values())), tuple(SIZES))
    dp = ("y", "z", "x")
    return jax.shard_map(
        on_device,
        mesh=grid,
        in_specs=(
            P(dp, None, "c"),
            P(dp, None, "c"),
            P("c", None),
            P(),
            P(dp, "c"),
            P(dp, "c"),
            P(dp, None),
            P(dp),
            P(dp),
        ),
        out_specs=(
            P(dp, None, "c"),
            P(dp, "c"),
            P(dp, "c"),
            P(None, "c"),
            P(dp),
            P(dp),
            P(),
        ),
        check_vma=False,
    )
```

time: 1860 us -> 135 us (0.07)
  blocking collectives: 1360 us -> 0 us
  waiting for transfers between devices: 455 us -> 64.8 us
  starting transfers between devices: 0.12 us -> 44.7 us
    unnamed x1 -> x0, blocking collectives: 682 us -> none
    psum x1 -> x0, blocking collectives: 677 us -> none  [on_device(): vec_total = lax.psum(vec_term, 'dp')]
    psum x2 -> x0, waiting for transfers between devices: 455 us -> none  [the longest x1 245 us: on_device(): row_total = lax.psum(row_part, ('dp', 'tensor'))]
    ppermute x0 -> x18, waiting for transfers between devices: none -> 45.9 us  [the longest x17 44.6 us: flips(): lax.ppermute(value, axis, [(i, i ^ d) for i in range(n)])]
    ppermute x0 -> x18, starting transfers between devices: none -> 24.1 us  [the longest x17 24 us: flips(): lax.ppermute(value, axis, [(i, i ^ d) for i in range(n)])]
    all_to_all x0 -> x2, starting transfers between devices: none -> 20.6 us  [on_device(): pieces = lax.all_to_all(pieces, ('z', 'x'), 0, 0, tiled=True)]
    all_to_all x0 -> x2, waiting for transfers between devices: none -> 18.9 us  [on_device(): pieces = lax.all_to_all(pieces, ('z', 'x'), 0, 0, tiled=True)]
  transfers between devices with their start and end apart: 3 -> 20, of which waited for: 2 -> 13; matrix products, arithmetic and copies ran while one was open for 0% -> 0% of each run, Pallas kernels for 0% -> 0%
where the time goes in v2:
time: 135 us; the launch traced here: 134 us
  waiting for transfers between devices  64.8 us (48%)
  starting transfers between devices  44.7 us (33%)
  Pallas kernels  12.3 us (9%)
  local copies, waits for them, and re-layouts  10.6 us (8%)
    ppermute x17, waiting for transfers between devices, flips(): lax.ppermute(value, axis, [(i, i ^ d) for i in range(n)])  44.6 us
    ppermute x17, starting transfers between devices, flips(): lax.ppermute(value, axis, [(i, i ^ d) for i in range(n)])  24 us
    all_to_all x2, starting transfers between devices, on_device(): pieces = lax.all_to_all(pieces, ('z', 'x'), 0, 0, tiled=True)  20.6 us
    all_to_all x2, waiting for transfers between devices, on_device(): pieces = lax.all_to_all(pieces, ('z', 'x'), 0, 0, tiled=True)  18.9 us
    unnamed x30, local copies, waits for them, and re-layouts  9.12 us
    pallas_call x1, Pallas kernels, apply_call(): pl.pallas_call(apply_kernel, grid_spec=pltpu.PrefetchScalarGridSpec(num_s...  5.35 us
    pallas_call x1, Pallas kernels, row_call(): pl.pallas_call(row_kernel, in_specs=[HBM] * 5, out_shape=[jax.ShapeDtypeS...  4.75 us
  transfers between devices with their start and end apart: 20, of which 13 were waited for; matrix products, arithmetic and copies ran while one was open for 0% of the time, Pallas kernels for 0%

profile of v2, /device:TPU:32, one launch (start us, length us, event | category | flops | bytes accessed | tf_op | source)
XLA Modules:
  0.0 134.2 jit_solution(9949148536121052177)
XLA Ops:
  0.6 1.7 %copy-done = bf16[1,768,1536]{2,1,0:T(8,128)(2,1)S(1)} copy-done((bf16[1,768,1536]{2,1,0:T(8,128)(2,1)S(1)}, bf16[1,768,1536]{2,1,0:T(8,128)(2,1)}, u32[]{:S(2)}) %copy-start) | copy-done | bytes 2359320
  2.3 1.7 %copy-done.1 = bf16[1,768,1536]{2,1,0:T(8,128)(2,1)S(1)} copy-done((bf16[1,768,1536]{2,1,0:T(8,128)(2,1)S(1)}, bf16[1,768,1536]{2,1,0:T(8,128)(2,1)}, u32[]{:S(2)}) %copy-start.1) | copy-done | bytes 2359320
  4.0 0.8 copy-done.6
  4.8 0.8 copy-done.8
  5.6 0.9 copy-done.10
  6.5 4.7 %row_sum.1 = (bf16[768,1536]{1,0:T(8,128)(2,1)S(1)}, f32[168,128]{1,0:T(8,128)S(1)}, f32[96,128]{1,0:T(8,128)S(1)}) custom-call(f32[32,1536]{1,0:T(8,128)S(1)} %bitcast.11, bf16[768,1536]{1,0:T(8,128)(2,1)S(1)} %bitcast.9, bf16[768,1536]{1,0:T(8,128)(2,1)S(1)} %bitcast.10, f32[6,1536]{1,0:T(8,128)S(1)} %copy-done.6, f32[6,1536]{1,0:T(8,128)S(1)} %copy-done.8), custom_call_target="tpu_custom_call" | custom-call | tf_op jit(solution)/shard_map/row_sum/pallas_call | solution.py:87
  11.3 0.0 copy-start.11
  11.3 0.1 collective-permute-start
  11.4 1.2 collective-permute-done
  12.6 5.5 %collective-permute-start.1 = (f32[168,128]{1,0:T(8,128)S(1)}, f32[168,128]{1,0:T(8,128)S(1)}, u32[]{:S(2)}, u32[]{:S(2)}) collective-permute-start(f32[168,128]{1,0:T(8,128)S(1)} %pad_add_fusion.own_ref), channel_id=1, source_target_pairs={{0,48},{8,56},{16,32},{24,40},{32,16},{40,24},{48,0},{56,8},{1,49}... | collective-permute-start | bytes 258056 | tf_op jit(solution)/shard_map/ppermute | solution.py:23
  18.1 4.7 %collective-permute-done.1.other_ref = f32[168,128]{1,0:T(8,128)S(1)} collective-permute-done((f32[168,128]{1,0:T(8,128)S(1)}, f32[168,128]{1,0:T(8,128)S(1)}, u32[]{:S(2)}, u32[]{:S(2)}) %collective-permute-start.1) | collective-permute-done | bytes 86048 | tf_op jit(solution)/shard_map/ppermute | solution.py:23
  22.8 1.1 collective-permute-start.4
  23.9 1.6 %collective-permute-start.3 = (f32[240,128]{1,0:T(8,128)S(1)}, f32[240,128]{1,0:T(8,128)S(1)}, u32[]{:S(2)}, u32[]{:S(2)}) collective-permute-start(f32[240,128]{1,0:T(8,128)S(1)} %pair_kernel.1.refs_0_), channel_id=1, source_target_pairs={{0,16},{8,24},{16,0},{24,8},{32,48},{40,56},{48,32},{56,40},{1,17}... | collective-permute-start | bytes 368648 | tf_op jit(solution)/shard_map/ppermute | solution.py:23
  25.5 0.9 collective-permute-start.2
  26.4 0.1 subtract_dynamic-update-slice_fusion
  26.5 0.1 convert_reduce_fusion
  26.6 7.0 %collective-permute-done.4.refs_3_ = f32[240,128]{1,0:T(8,128)S(1)} collective-permute-done((f32[240,128]{1,0:T(8,128)S(1)}, f32[240,128]{1,0:T(8,128)S(1)}, u32[]{:S(2)}, u32[]{:S(2)}) %collective-permute-start.4) | collective-permute-done | bytes 122912 | tf_op jit(solution)/shard_map/ppermute | solution.py:23
  33.6 0.6 collective-permute-done.3.refs_2_
  34.2 0.0 collective-permute-done.2.refs_1_
  34.2 2.8 %collective-permute-start.7 = (bf16[864,128]{1,0:T(8,128)(2,1)S(1)}, bf16[864,128]{1,0:T(8,128)(2,1)S(1)}, u32[]{:S(2)}, u32[]{:S(2)}) collective-permute-start(bf16[864,128]{1,0:T(8,128)(2,1)S(1)} %spread_kernel.1.refs_0_), channel_id=1, source_target_pairs={{0,6},{2,4},{4,2},{6,0},{1,7},{3,5},{5,3},{7,1},{8,14},{10,12},{12... | collective-permute-start | bytes 663560 | tf_op jit(solution)/shard_map/ppermute | solution.py:23
  37.1 0.8 collective-permute-start.6
  37.9 0.5 collective-permute-start.5
  38.4 8.7 %collective-permute-done.7.refs_3_ = bf16[864,128]{1,0:T(8,128)(2,1)S(1)} collective-permute-done((bf16[864,128]{1,0:T(8,128)(2,1)S(1)}, bf16[864,128]{1,0:T(8,128)(2,1)S(1)}, u32[]{:S(2)}, u32[]{:S(2)}) %collective-permute-start.7) | collective-permute-done | bytes 221216 | tf_op jit(solution)/shard_map/ppermute | solution.py:23
  47.1 0.0 collective-permute-done.6.refs_2_
  47.2 0.7 copy-done.2
  47.8 0.0 collective-permute-done.5.refs_1_
  47.8 0.7 copy-done.4
  48.5 0.9 copy-done.3
  49.5 0.9 copy-done.5
  50.4 0.1 collect_kernel.1
  50.5 0.0 copy-start.7
  50.5 0.0 copy-start.9
  50.5 3.1 %collective-permute-start.10 = (f32[96,128]{1,0:T(8,128)S(1)}, f32[96,128]{1,0:T(8,128)S(1)}, u32[]{:S(2)}, u32[]{:S(2)}) collective-permute-start(f32[96,128]{1,0:T(8,128)S(1)} %get-tuple-element.31), channel_id=1, source_target_pairs={{0,192},{64,128},{128,64},{192,0},{1,193},{65,129},{129,65},{193,1... | collective-permute-start | bytes 147464 | tf_op jit(solution)/shard_map/ppermute | solution.py:23
  53.6 0.6 collective-permute-start.9
  54.2 0.5 collective-permute-start.8
  54.7 1.2 collective-permute-done.10
  55.9 3.3 %collective-permute-done.9 = f32[96,128]{1,0:T(8,128)S(1)} collective-permute-done((f32[96,128]{1,0:T(8,128)S(1)}, f32[96,128]{1,0:T(8,128)S(1)}, u32[]{:S(2)}, u32[]{:S(2)}) %collective-permute-start.9) | collective-permute-done | bytes 49184 | tf_op jit(solution)/shard_map/ppermute | solution.py:23
  59.2 0.0 collective-permute-done.8
  59.2 0.1 collective-permute-start.11
  59.3 1.2 collective-permute-done.11.other_ref
  60.5 0.0 copy-done.11
  60.5 2.1 %column_sum.1 = (f32[4,32,192]{2,1,0:T(8,128)S(1)}, f32[32,15,128]{2,1,0:T(8,128)}) custom-call(f32[96,128]{1,0:T(8,128)S(1)} %add_add_fusion.own_ref, f32[96,128]{1,0:T(8,128)S(1)} %collective-permute-done.11.other_ref, f32[32,32]{1,0:T(8,128)S(1)} %copy-done.11, bf16[768,1536]{1,0:T(8,128)(2,1)S(1)} %get-tuple-element.35.merged_ref, ...), custom_call_target="tpu_custom_call" | custom-call | tf_op jit(solution)/shard_map/column_sum/pallas_call | solution.py:187
  62.7 10.8 %all-to-all-start = ((f32[32,15,128]{2,1,0:T(8,128)}), f32[32,15,128]{2,1,0:T(8,128)S(1)}, u32[]{:S(2)}, u32[]{:S(2)}) async-start(f32[32,15,128]{2,1,0:T(8,128)} %get-tuple-element.38), calls=%async_computation | async-start | bytes 524288 | tf_op jit(solution)/shard_map/all_to_all | solution.py:373
  73.5 1.4 %collective-permute-start.17 = (bf16[2304,128]{1,0:T(8,128)(2,1)S(1)}, bf16[2304,128]{1,0:T(8,128)(2,1)}, u32[]{:S(2)}, u32[]{:S(2)}) collective-permute-start(bf16[2304,128]{1,0:T(8,128)(2,1)S(1)} %get-tuple-element.41.base0), channel_id=1, source_target_pairs={{0,192},{64,128},{128,64},{192,0},{1,193},{65,129},{129,65},{193,1... | collective-permute-start | bytes 1769480 | tf_op jit(solution)/shard_map/ppermute | solution.py:23
  74.9 0.9 collective-permute-start.16
  75.8 1.9 %collective-permute-start.15 = (bf16[2304,128]{1,0:T(8,128)(2,1)S(1)}, bf16[2304,128]{1,0:T(8,128)(2,1)}, u32[]{:S(2)}, u32[]{:S(2)}) collective-permute-start(bf16[2304,128]{1,0:T(8,128)(2,1)S(1)} %get-tuple-element.41.base0), channel_id=1, source_target_pairs={{0,64},{64,0},{128,192},{192,128},{1,65},{65,1},{129,193},{193,129... | collective-permute-start | bytes 1769480 | tf_op jit(solution)/shard_map/ppermute | solution.py:23
  77.7 8.3 %all-to-all-done = f32[32,15,128]{2,1,0:T(8,128)S(1)} async-done(((f32[32,15,128]{2,1,0:T(8,128)}), f32[32,15,128]{2,1,0:T(8,128)S(1)}, u32[]{:S(2)}, u32[]{:S(2)}) %all-to-all-start) | async-done | bytes 245792 | tf_op jit(solution)/shard_map/all_to_all | solution.py:373
  86.0 1.4 %collective-permute-start.14 = (f32[15,128]{1,0:T(8,128)S(1)}, f32[15,128]{1,0:T(8,128)S(1)}, u32[]{:S(2)}, u32[]{:S(2)}) collective-permute-start(f32[15,128]{1,0:T(8,128)S(1)} %reduce_sum.9), channel_id=1, source_target_pairs={{0,192},{64,128},{128,64},{192,0},{1,193},{65,129},{129,65},{193,1... | collective-permute-start | bytes 23048 | tf_op jit(solution)/shard_map/ppermute | solution.py:23
  87.4 0.9 collective-permute-start.13
  88.3 14.2 %collective-permute-done.14 = f32[15,128]{1,0:T(8,128)S(1)} collective-permute-done((f32[15,128]{1,0:T(8,128)S(1)}, f32[15,128]{1,0:T(8,128)S(1)}, u32[]{:S(2)}, u32[]{:S(2)}) %collective-permute-start.14) | collective-permute-done | bytes 7712 | tf_op jit(solution)/shard_map/ppermute | solution.py:23
  102.6 0.0 collective-permute-start.12
  102.6 1.3 collective-permute-done.13
  103.8 2.4 %collective-permute-done.12 = f32[15,128]{1,0:T(8,128)S(1)} collective-permute-done((f32[15,128]{1,0:T(8,128)S(1)}, f32[15,128]{1,0:T(8,128)S(1)}, u32[]{:S(2)}, u32[]{:S(2)}) %collective-permute-start.12) | collective-permute-done | bytes 7712 | tf_op jit(solution)/shard_map/ppermute | solution.py:23
  106.2 0.0 collective-permute-done.17.base3
  106.2 0.0 collective-permute-done.16.base2
  106.2 0.0 collective-permute-done.15.base1
  106.2 0.7 broadcast_in_dim.13
  107.0 9.8 %all-to-all-start.1 = ((f32[32,15,128]{2,1,0:T(8,128)}), f32[32,15,128]{2,1,0:T(8,128)S(1)}, u32[]{:S(2)}, u32[]{:S(2)}) async-start(f32[32,15,128]{2,1,0:T(8,128)} %broadcast_in_dim.13), calls=%async_computation.1 | async-start | bytes 524288 | tf_op jit(solution)/shard_map/all_to_all | solution.py:377
  116.8 0.1 pad_add_fusion.1.where
  116.8 0.1 dynamic-slice_bitcast_fusion.own_basis_ref
  116.9 10.6 %all-to-all-done.1.piece_ref = f32[32,15,128]{2,1,0:T(8,128)S(1)} async-done(((f32[32,15,128]{2,1,0:T(8,128)}), f32[32,15,128]{2,1,0:T(8,128)S(1)}, u32[]{:S(2)}, u32[]{:S(2)}) %all-to-all-start.1) | async-done | bytes 245792 | tf_op jit(solution)/shard_map/all_to_all | solution.py:377
  127.6 0.6 convert_element_type.19
  128.2 0.6 multiply_subtract_fusion
  128.8 5.3 %apply.1 = (bf16[768,1536]{1,0:T(8,128)(2,1)}, bf16[768,1536]{1,0:T(8,128)(2,1)}, f32[6,1536]{1,0:T(8,128)}, f32[6,1536]{1,0:T(8,128)}) custom-call(s32[3]{0:T(128)S(1)} %pad_add_fusion.1.where, f32[32,6]{1,0:T(8,128)S(1)} %dynamic-slice_bitcast_fusion.own_basis_ref, f32[32,15,128]{2,1,0:T(8,128)S(1)} %all-to-all-done.1.piece_ref, ...), custom_call_target="tpu_custom_call" | custom-call | tf_op jit(solution)/shard_map/apply/pallas_call | solution.py:279
  (28 shorter events, 0.2 us)
Async XLA Ops:
  0.6 1.7 %copy-start = (bf16[1,768,1536]{2,1,0:T(8,128)(2,1)S(1)}, bf16[1,768,1536]{2,1,0:T(8,128)(2,1)}, u32[]{:S(2)}) copy-start(bf16[1,768,1536]{2,1,0:T(8,128)(2,1)} %param.9) | copy-start | bytes 7077892
  2.3 1.7 %copy-start.1 = (bf16[1,768,1536]{2,1,0:T(8,128)(2,1)S(1)}, bf16[1,768,1536]{2,1,0:T(8,128)(2,1)}, u32[]{:S(2)}) copy-start(bf16[1,768,1536]{2,1,0:T(8,128)(2,1)} %param.10) | copy-start | bytes 7077892
  4.0 0.8 copy-start.6
  4.8 0.8 copy-start.8
  5.6 0.9 copy-start.10
  6.5 19.9 %copy-start.13 = (f32[42]{0:T(128)S(1)}, f32[42]{0:T(128)}, u32[]{:S(2)}) copy-start(f32[42]{0:T(128)} %param.16) | copy-start | bytes 508
  6.5 19.9 %copy-start.14 = (f32[42]{0:T(128)S(1)}, f32[42]{0:T(128)}, u32[]{:S(2)}) copy-start(f32[42]{0:T(128)} %param.17) | copy-start | bytes 508
  6.5 20.0 %copy-start.12 = (bf16[1,5376]{1,0:T(2,128)(2,1)S(1)}, bf16[1,5376]{1,0:T(2,128)(2,1)}, u32[]{:S(2)}) copy-start(bf16[1,5376]{1,0:T(2,128)(2,1)} %param.15) | copy-start | bytes 32260
  11.3 49.3 %copy-start.11 = (f32[32,32]{1,0:T(8,128)S(1)}, f32[32,32]{1,0:T(8,128)}, u32[]{:S(2)}) copy-start(f32[32,32]{1,0:T(8,128)} %gram_ref.1) | copy-start | bytes 12292
  11.3 1.3 collective-permute-start
  12.6 10.2 %collective-permute-start.1 = (f32[168,128]{1,0:T(8,128)S(1)}, f32[168,128]{1,0:T(8,128)S(1)}, u32[]{:S(2)}, u32[]{:S(2)}) collective-permute-start(f32[168,128]{1,0:T(8,128)S(1)} %pad_add_fusion.own_ref), channel_id=1, source_target_pairs={{0,48},{8,56},{16,32},{24,40},{32,16},{40,24},{48,0},{56,8},{1,49}... | collective-permute-start | bytes 258056 | tf_op jit(solution)/shard_map/ppermute | solution.py:23
  22.8 10.8 %collective-permute-start.4 = (f32[240,128]{1,0:T(8,128)S(1)}, f32[240,128]{1,0:T(8,128)S(1)}, u32[]{:S(2)}, u32[]{:S(2)}) collective-permute-start(f32[240,128]{1,0:T(8,128)S(1)} %pair_kernel.1.refs_0_), channel_id=1, source_target_pairs={{0,24},{8,16},{16,8},{24,0},{32,56},{40,48},{48,40},{56,32},{1,25}... | collective-permute-start | bytes 368648 | tf_op jit(solution)/shard_map/ppermute | solution.py:23
  23.9 10.3 %collective-permute-start.3 = (f32[240,128]{1,0:T(8,128)S(1)}, f32[240,128]{1,0:T(8,128)S(1)}, u32[]{:S(2)}, u32[]{:S(2)}) collective-permute-start(f32[240,128]{1,0:T(8,128)S(1)} %pair_kernel.1.refs_0_), channel_id=1, source_target_pairs={{0,16},{8,24},{16,0},{24,8},{32,48},{40,56},{48,32},{56,40},{1,17}... | collective-permute-start | bytes 368648 | tf_op jit(solution)/shard_map/ppermute | solution.py:23
  25.5 8.7 %collective-permute-start.2 = (f32[240,128]{1,0:T(8,128)S(1)}, f32[240,128]{1,0:T(8,128)S(1)}, u32[]{:S(2)}, u32[]{:S(2)}) collective-permute-start(f32[240,128]{1,0:T(8,128)S(1)} %pair_kernel.1.refs_0_), channel_id=1, source_target_pairs={{0,8},{8,0},{16,24},{24,16},{32,40},{40,32},{48,56},{56,48},{1,9},... | collective-permute-start | bytes 368648 | tf_op jit(solution)/shard_map/ppermute | solution.py:23
  34.2 12.9 %collective-permute-start.7 = (bf16[864,128]{1,0:T(8,128)(2,1)S(1)}, bf16[864,128]{1,0:T(8,128)(2,1)S(1)}, u32[]{:S(2)}, u32[]{:S(2)}) collective-permute-start(bf16[864,128]{1,0:T(8,128)(2,1)S(1)} %spread_kernel.1.refs_0_), channel_id=1, source_target_pairs={{0,6},{2,4},{4,2},{6,0},{1,7},{3,5},{5,3},{7,1},{8,14},{10,12},{12... | collective-permute-start | bytes 663560 | tf_op jit(solution)/shard_map/ppermute | solution.py:23
  37.1 10.1 %collective-permute-start.6 = (bf16[864,128]{1,0:T(8,128)(2,1)S(1)}, bf16[864,128]{1,0:T(8,128)(2,1)S(1)}, u32[]{:S(2)}, u32[]{:S(2)}) collective-permute-start(bf16[864,128]{1,0:T(8,128)(2,1)S(1)} %spread_kernel.1.refs_0_), channel_id=1, source_target_pairs={{0,4},{2,6},{4,0},{6,2},{1,5},{3,7},{5,1},{7,3},{8,12},{10,14},{12... | collective-permute-start | bytes 663560 | tf_op jit(solution)/shard_map/ppermute | solution.py:23
  37.9 10.0 %collective-permute-start.5 = (bf16[864,128]{1,0:T(8,128)(2,1)S(1)}, bf16[864,128]{1,0:T(8,128)(2,1)S(1)}, u32[]{:S(2)}, u32[]{:S(2)}) collective-permute-start(bf16[864,128]{1,0:T(8,128)(2,1)S(1)} %spread_kernel.1.refs_0_), channel_id=1, source_target_pairs={{0,2},{2,0},{4,6},{6,4},{1,3},{3,1},{5,7},{7,5},{8,10},{10,8},{12,... | collective-permute-start | bytes 663560 | tf_op jit(solution)/shard_map/ppermute | solution.py:23
  47.2 0.7 copy-start.2
  47.8 0.7 copy-start.4
  48.5 0.9 copy-start.3
  49.5 0.9 copy-start.5
  50.5 78.3 %copy-start.7 = (f32[6,1536]{1,0:T(8,128)S(1)}, f32[6,1536]{1,0:T(8,128)}, u32[]{:S(2)}) copy-start(f32[6,1536]{1,0:T(8,128)} %master_hbm.3) | copy-start | bytes 110596
  50.5 78.3 %copy-start.9 = (f32[6,1536]{1,0:T(8,128)S(1)}, f32[6,1536]{1,0:T(8,128)}, u32[]{:S(2)}) copy-start(f32[6,1536]{1,0:T(8,128)} %momentum_hbm.3) | copy-start | bytes 110596
  50.5 5.4 %collective-permute-start.10 = (f32[96,128]{1,0:T(8,128)S(1)}, f32[96,128]{1,0:T(8,128)S(1)}, u32[]{:S(2)}, u32[]{:S(2)}) collective-permute-start(f32[96,128]{1,0:T(8,128)S(1)} %get-tuple-element.31), channel_id=1, source_target_pairs={{0,192},{64,128},{128,64},{192,0},{1,193},{65,129},{129,65},{193,1... | collective-permute-start | bytes 147464 | tf_op jit(solution)/shard_map/ppermute | solution.py:23
  53.6 5.6 %collective-permute-start.9 = (f32[96,128]{1,0:T(8,128)S(1)}, f32[96,128]{1,0:T(8,128)S(1)}, u32[]{:S(2)}, u32[]{:S(2)}) collective-permute-start(f32[96,128]{1,0:T(8,128)S(1)} %get-tuple-element.31), channel_id=1, source_target_pairs={{0,128},{64,192},{128,0},{192,64},{1,129},{65,193},{129,1},{193,65... | collective-permute-start | bytes 147464 | tf_op jit(solution)/shard_map/ppermute | solution.py:23
  54.2 5.0 %collective-permute-start.8 = (f32[96,128]{1,0:T(8,128)S(1)}, f32[96,128]{1,0:T(8,128)S(1)}, u32[]{:S(2)}, u32[]{:S(2)}) collective-permute-start(f32[96,128]{1,0:T(8,128)S(1)} %get-tuple-element.31), channel_id=1, source_target_pairs={{0,64},{64,0},{128,192},{192,128},{1,65},{65,1},{129,193},{193,129... | collective-permute-start | bytes 147464 | tf_op jit(solution)/shard_map/ppermute | solution.py:23
  59.2 1.3 collective-permute-start.11
  62.7 23.3 %all-to-all-start = ((f32[32,15,128]{2,1,0:T(8,128)}), f32[32,15,128]{2,1,0:T(8,128)S(1)}, u32[]{:S(2)}, u32[]{:S(2)}) async-start(f32[32,15,128]{2,1,0:T(8,128)} %get-tuple-element.38), calls=%async_computation | async-start | bytes 524288 | tf_op jit(solution)/shard_map/all_to_all | solution.py:373
  73.5 32.7 %collective-permute-start.17 = (bf16[2304,128]{1,0:T(8,128)(2,1)S(1)}, bf16[2304,128]{1,0:T(8,128)(2,1)}, u32[]{:S(2)}, u32[]{:S(2)}) collective-permute-start(bf16[2304,128]{1,0:T(8,128)(2,1)S(1)} %get-tuple-element.41.base0), channel_id=1, source_target_pairs={{0,192},{64,128},{128,64},{192,0},{1,193},{65,129},{129,65},{193,1... | collective-permute-start | bytes 1769480 | tf_op jit(solution)/shard_map/ppermute | solution.py:23
  74.9 31.3 %collective-permute-start.16 = (bf16[2304,128]{1,0:T(8,128)(2,1)S(1)}, bf16[2304,128]{1,0:T(8,128)(2,1)}, u32[]{:S(2)}, u32[]{:S(2)}) collective-permute-start(bf16[2304,128]{1,0:T(8,128)(2,1)S(1)} %get-tuple-element.41.base0), channel_id=1, source_target_pairs={{0,128},{64,192},{128,0},{192,64},{1,129},{65,193},{129,1},{193,65... | collective-permute-start | bytes 1769480 | tf_op jit(solution)/shard_map/ppermute | solution.py:23
  75.8 30.4 %collective-permute-start.15 = (bf16[2304,128]{1,0:T(8,128)(2,1)S(1)}, bf16[2304,128]{1,0:T(8,128)(2,1)}, u32[]{:S(2)}, u32[]{:S(2)}) collective-permute-start(bf16[2304,128]{1,0:T(8,128)(2,1)S(1)} %get-tuple-element.41.base0), channel_id=1, source_target_pairs={{0,64},{64,0},{128,192},{192,128},{1,65},{65,1},{129,193},{193,129... | collective-permute-start | bytes 1769480 | tf_op jit(solution)/shard_map/ppermute | solution.py:23
  86.0 16.5 %collective-permute-start.14 = (f32[15,128]{1,0:T(8,128)S(1)}, f32[15,128]{1,0:T(8,128)S(1)}, u32[]{:S(2)}, u32[]{:S(2)}) collective-permute-start(f32[15,128]{1,0:T(8,128)S(1)} %reduce_sum.9), channel_id=1, source_target_pairs={{0,192},{64,128},{128,64},{192,0},{1,193},{65,129},{129,65},{193,1... | collective-permute-start | bytes 23048 | tf_op jit(solution)/shard_map/ppermute | solution.py:23
  87.4 16.4 %collective-permute-start.13 = (f32[15,128]{1,0:T(8,128)S(1)}, f32[15,128]{1,0:T(8,128)S(1)}, u32[]{:S(2)}, u32[]{:S(2)}) collective-permute-start(f32[15,128]{1,0:T(8,128)S(1)} %reduce_sum.9), channel_id=1, source_target_pairs={{0,128},{64,192},{128,0},{192,64},{1,129},{65,193},{129,1},{193,65... | collective-permute-start | bytes 23048 | tf_op jit(solution)/shard_map/ppermute | solution.py:23
  102.6 3.7 %collective-permute-start.12 = (f32[15,128]{1,0:T(8,128)S(1)}, f32[15,128]{1,0:T(8,128)S(1)}, u32[]{:S(2)}, u32[]{:S(2)}) collective-permute-start(f32[15,128]{1,0:T(8,128)S(1)} %reduce_sum.9), channel_id=1, source_target_pairs={{0,64},{64,0},{128,192},{192,128},{1,65},{65,1},{129,193},{193,129... | collective-permute-start | bytes 23048 | tf_op jit(solution)/shard_map/ppermute | solution.py:23
  107.0 20.6 %all-to-all-start.1 = ((f32[32,15,128]{2,1,0:T(8,128)}), f32[32,15,128]{2,1,0:T(8,128)S(1)}, u32[]{:S(2)}, u32[]{:S(2)}) async-start(f32[32,15,128]{2,1,0:T(8,128)} %broadcast_in_dim.13), calls=%async_computation.1 | async-start | bytes 524288 | tf_op jit(solution)/shard_map/all_to_all | solution.py:377

commit v3 on v2

--- a/solution.py
+++ b/solution.py
@@ -39,8 +39,8 @@
 
 
 def row_kernel(
-    query_hbm, grads_hbm, error_hbm, master_hbm, momentum_hbm, merged_ref, payload_ref, other_ref,
-    query, grads, error, master, momentum, sems,
+    query_hbm, grads_hbm, error_hbm, master_hbm, momentum_hbm, merged_hbm, payload_ref, other_ref,
+    query, grads, error, master, momentum, merged_blocks, sems, out_sems,
 ):
     n_blocks = grads_hbm.shape[0] // LANES
     copies = [pltpu.make_async_copy(query_hbm, query, sems.at[0])]
@@ -56,12 +56,15 @@
     query_b = query[...].astype(jnp.bfloat16)
     first = lax.axis_index("c") == 0
     half = query_b.shape[0] // 2
+    leaving = []
     for i in range(n_blocks):
         at = pl.ds(i * LANES, LANES)
         copies[1 + 2 * i].wait()
         copies[2 + 2 * i].wait()
         merged = merge(grads[at, :], error[at, :])
-        merged_ref[at, :] = merged
+        merged_blocks[at, :] = merged
+        leaving.append(pltpu.make_async_copy(merged_blocks.at[at], merged_hbm.at[at], out_sems.at[i]))
+        leaving[i].start()
         part = lax.dot_general(
             query_b, merged, (((1,), (1,)), ((), ())), preferred_element_type=jnp.float32
         )
@@ -77,6 +80,8 @@
         for g in range(groups):
             row = n_sums + r * groups + g
             payload_ref[row : row + 1, :] = base[r : r + 1, g * LANES : (g + 1) * LANES]
+    for copy in leaving:
+        copy.wait()
 
 
 def row_call(query_t, grads, error, master, momentum):
@@ -87,6 +92,7 @@
     return pl.pallas_call(
         row_kernel,
         in_specs=[HBM] * 5,
+        out_specs=[HBM] + [pl.BlockSpec(memory_space=pltpu.VMEM)] * 2,
         out_shape=[
             jax.ShapeDtypeStruct(grads.shape, jnp.bfloat16),
             jax.ShapeDtypeStruct((n_sums + n_base, LANES), jnp.float32),
@@ -98,44 +104,54 @@
             pltpu.VMEM(grads.shape, jnp.bfloat16),
             pltpu.VMEM(master.shape, jnp.float32),
             pltpu.VMEM(master.shape, jnp.float32),
+            pltpu.VMEM(grads.shape, jnp.bfloat16),
             pltpu.SemaphoreType.DMA((3 + 2 * (rows // LANES),)),
+            pltpu.SemaphoreType.DMA((rows // LANES,)),
         ],
-        compiler_params=pltpu.CompilerParams(vmem_limit_bytes=VMEM),
+        compiler_params=pltpu.CompilerParams(vmem_limit_bytes=60 << 20),
         name="row_sum",
     )(query_t, grads, error, master, momentum)
 
 
-def pair_kernel(n_sums, own_ref, other_ref, out_ref):
-    n = own_ref.shape[0] - n_sums
-    out_ref[:n_sums, :] = own_ref[:n_sums, :] + other_ref[:n_sums, :]
-    out_ref[n_sums : n_sums + n, :] = own_ref[n_sums:, :]
-    out_ref[n_sums + n :, :] = other_ref[n_sums:, :]
-
-
-def spread_kernel(n_sums, *refs):
+def split(value):
+    high = value.astype(jnp.bfloat16)
+    return high, (value - high.astype(jnp.float32)).astype(jnp.bfloat16)
+
+
+def first_kernel(n_sums, own_ref, other_ref, out_ref):
+    high, low = split(own_ref[:n_sums, :] + other_ref[...])
+    out_ref[:n_sums, :] = high
+    out_ref[n_sums : 2 * n_sums, :] = low
+    out_ref[2 * n_sums :, :] = own_ref[n_sums:, :].astype(jnp.bfloat16)
+
+
+def sums_of(block, n_sums):
+    return block[:n_sums].astype(jnp.float32) + block[n_sums : 2 * n_sums].astype(jnp.float32)
+
+
+def stage_kernel(n_sums, *refs):
     *blocks, out_ref = refs
-    for k, term in enumerate(thirds(total([b[:n_sums, :] for b in blocks]))):
-        out_ref[k * n_sums : (k + 1) * n_sums, :] = term
-    n = blocks[0].shape[0] - n_sums
+    high, low = split(total([sums_of(b[: 2 * n_sums, :], n_sums) for b in blocks]))
+    out_ref[:n_sums, :] = high
+    out_ref[n_sums : 2 * n_sums, :] = low
+    n = blocks[0].shape[0] - 2 * n_sums
     for j, b in enumerate(blocks):
-        first = 3 * n_sums + j * n
-        out_ref[first : first + n, :] = b[n_sums:, :].astype(jnp.bfloat16)
-
-
-def collect_kernel(n_sums, *refs):
-    *blocks, sums_ref, base_ref = refs
-    term = lambda b, k: b[k * n_sums : (k + 1) * n_sums, :].astype(jnp.float32)
-    sums_ref[...] = total([term(b, 0) + (term(b, 1) + term(b, 2)) for b in blocks])
-    n = blocks[0].shape[0] - 3 * n_sums
+        first = 2 * n_sums + j * n
+        out_ref[first : first + n, :] = b[2 * n_sums :, :]
+
+
+def join_kernel(n_sums, *refs):
+    *blocks, out_ref = refs
+    n = blocks[0].shape[0] - 2 * n_sums
     for j, b in enumerate(blocks):
-        base_ref[j * n : (j + 1) * n, :] = b[3 * n_sums :, :]
+        out_ref[j * n : (j + 1) * n, :] = b[2 * n_sums :, :]
 
 
 def blocks_call(kernel, blocks, n_sums, out_shape):
     return pl.pallas_call(
         functools.partial(kernel, n_sums),
         out_shape=out_shape,
-        compiler_params=pltpu.CompilerParams(vmem_limit_bytes=VMEM),
+        compiler_params=pltpu.CompilerParams(vmem_limit_bytes=8 << 20),
         name=kernel.__name__,
     )(*blocks)
 
@@ -299,7 +315,7 @@
             jax.ShapeDtypeStruct(master.shape, jnp.float32),
             jax.ShapeDtypeStruct(master.shape, jnp.float32),
         ],
-        compiler_params=pltpu.CompilerParams(vmem_limit_bytes=VMEM),
+        compiler_params=pltpu.CompilerParams(vmem_limit_bytes=60 << 20),
         name="apply",
     )(where, own_basis, pieces, merged, row_basis, *bases, master, momentum)
 
@@ -336,24 +352,16 @@
     merged, payload, row_other = row_call(query.T, grads, error, fc_master, fc_momentum)
     n_sums = row_other.shape[0]
     row_other = lax.ppermute(row_other, "c", [(0, 1), (1, 0)])
-    payload = payload + jnp.pad(row_other, ((0, payload.shape[0] - n_sums), (0, 0)))
     n_base = payload.shape[0] - n_sums
-    lanes = lambda rows, dtype: jax.ShapeDtypeStruct((rows, LANES), dtype)
-    payload = blocks_call(
-        pair_kernel, flips(payload, "z", (0, 6)), n_sums, lanes(n_sums + 2 * n_base, jnp.float32)
-    )
-    payload = blocks_call(
-        spread_kernel,
-        flips(payload, "z", (0, 1, 2, 3)),
-        n_sums,
-        lanes(3 * n_sums + 8 * n_base, jnp.bfloat16),
-    )
-    sums, base = blocks_call(
-        collect_kernel,
-        flips(payload, "x"),
-        n_sums,
-        [lanes(n_sums, jnp.float32), lanes(32 * n_base, jnp.bfloat16)],
-    )
+    lanes = lambda rows: jax.ShapeDtypeStruct((rows, LANES), jnp.bfloat16)
+    payload = blocks_call(first_kernel, (payload, row_other), n_sums, lanes(2 * n_sums + n_base))
+    blocks = flips(payload, "z", (0, 6))
+    payload = blocks_call(stage_kernel, blocks, n_sums, lanes(2 * n_sums + 2 * n_base))
+    blocks = flips(payload, "z", (0, 1, 2, 3))
+    payload = blocks_call(stage_kernel, blocks, n_sums, lanes(2 * n_sums + 8 * n_base))
+    blocks = flips(payload, "x")
+    sums = total([sums_of(b, n_sums) for b in blocks])
+    base = blocks_call(join_kernel, blocks, n_sums, lanes(32 * n_base))
     vec = vec_rows_of(rank, replica_index, vec_grads, vec_master, vec_momentum)
     sums, vec = lax.optimization_barrier((sums, vec))
     sums = total(flips(sums, "y"))
@@ -371,8 +379,8 @@
     )[0]
 
     pieces = lax.all_to_all(pieces, ("z", "x"), 0, 0, tiled=True)
-    piece = total(flips(jnp.sum(pieces, 0), "y"))
-    piece, *bases = lax.optimization_barrier((piece, *bases))
+    piece, *bases = lax.optimization_barrier((jnp.sum(pieces, 0), *bases))
+    piece = total(flips(piece, "y"))
     pieces = jnp.broadcast_to(piece[None], (rank,) + piece.shape)
     pieces = lax.all_to_all(pieces, ("z", "x"), 0, 0, tiled=True)
 

time: 135 us -> 110 us (0.81)
  waiting for transfers between devices: 64.8 us -> 31.9 us
  blocking collectives: 0 us -> 22.9 us
  starting transfers between devices: 44.7 us -> 33.3 us
  local copies, waits for them, and re-layouts: 10.6 us -> 5.43 us
    ppermute x17, waiting for transfers between devices: 44.6 us -> 21 us  [flips(): lax.ppermute(value, axis, [(i, i ^ d) for i in range(n)])]
    all_to_all x0 -> x1, blocking collectives: none -> 22.9 us  [on_device(): pieces = lax.all_to_all(pieces, ('z', 'x'), 0, 0, tiled=True)]
    all_to_all x2 -> x1, starting transfers between devices: 20.6 us -> 7.36 us  [on_device(): pieces = lax.all_to_all(pieces, ('z', 'x'), 0, 0, tiled=True)]
    all_to_all x2 -> x1, waiting for transfers between devices: 18.9 us -> 9.52 us  [on_device(): pieces = lax.all_to_all(pieces, ('z', 'x'), 0, 0, tiled=True)]
    unnamed x30 -> x28, local copies, waits for them, and re-layouts: 9.12 us -> 2.71 us
    pallas_call x1, Pallas kernels: 5.35 us -> 7.46 us  [apply_call(): pl.pallas_call(apply_kernel, grid_spec=pltpu.PrefetchScalarGridSpec(num_s...]
    ppermute x17, starting transfers between devices: 24 us -> 25.9 us  [flips(): lax.ppermute(value, axis, [(i, i ^ d) for i in range(n)])]
  transfers between devices with their start and end apart: 20 -> 19, of which waited for: 13 -> 9; matrix products, arithmetic and copies ran while one was open for 0% -> 2% of each run, Pallas kernels for 0% -> 1%
where the time goes in v3:
time: 110 us
  starting transfers between devices  33.3 us (30%)
  waiting for transfers between devices  31.9 us (29%)
  blocking collectives  22.9 us (21%)
  Pallas kernels  13.6 us (12%)
  local copies, waits for them, and re-layouts  5.43 us (5%)
  other arithmetic  1.49 us (1%)
    ppermute x17, starting transfers between devices, flips(): lax.ppermute(value, axis, [(i, i ^ d) for i in range(n)])  25.9 us
    all_to_all x1, blocking collectives, on_device(): pieces = lax.all_to_all(pieces, ('z', 'x'), 0, 0, tiled=True)  22.9 us
    ppermute x17, waiting for transfers between devices, flips(): lax.ppermute(value, axis, [(i, i ^ d) for i in range(n)])  21 us
    all_to_all x1, waiting for transfers between devices, on_device(): pieces = lax.all_to_all(pieces, ('z', 'x'), 0, 0, tiled=True)  9.52 us
    pallas_call x1, Pallas kernels, apply_call(): pl.pallas_call(apply_kernel, grid_spec=pltpu.PrefetchScalarGridSpec(num_s...  7.46 us
    all_to_all x1, starting transfers between devices, on_device(): pieces = lax.all_to_all(pieces, ('z', 'x'), 0, 0, tiled=True)  7.36 us
    pallas_call x1, Pallas kernels, row_call(): pl.pallas_call(row_kernel, in_specs=[HBM] * 5, out_specs=[HBM] + [pl.Bloc...  4.6 us
    unnamed x28, local copies, waits for them, and re-layouts  2.71 us
  transfers between devices with their start and end apart: 19, of which 9 were waited for; matrix products, arithmetic and copies ran while one was open for 2% of the time, Pallas kernels for 1%

profile of v3, /device:TPU:32, one launch (start us, length us, event | category | flops | bytes accessed | tf_op | source)
XLA Modules:
  0.0 109.6 jit_solution(10580589386049285241)
XLA Ops:
  0.6 0.0 copy-start.10
  0.6 0.0 copy-start.12
  0.7 0.0 copy-start.9
  0.7 0.0 copy-start.7
  0.7 4.6 %row_sum.1 = (bf16[768,1536]{1,0:T(8,128)(2,1)}, f32[168,128]{1,0:T(8,128)}, f32[96,128]{1,0:T(8,128)}) custom-call(f32[32,1536]{1,0:T(8,128)} %bitcast.11, bf16[768,1536]{1,0:T(8,128)(2,1)} %bitcast.9, bf16[768,1536]{1,0:T(8,128)(2,1)} %bitcast.10, f32[6,1536]{1,0:T(8,128)} %master_hbm.3, f32[6,1536]{1,0:T(8,128)} %momentum_hbm.3), custom_call_target="tpu_custom_call" | custom-call | tf_op jit(solution)/shard_map/row_sum/pallas_call | solution.py:92
  5.3 0.1 collective-permute-start
  5.4 1.4 %collective-permute-done.other_ref = f32[96,128]{1,0:T(8,128)S(1)} collective-permute-done((f32[96,128]{1,0:T(8,128)}, f32[96,128]{1,0:T(8,128)S(1)}, u32[]{:S(2)}, u32[]{:S(2)}) %collective-permute-start) | collective-permute-done | bytes 49184 | tf_op jit(solution)/shard_map/ppermute | solution.py:354
  6.8 0.9 copy-done.6
  7.7 5.5 %collective-permute-start.1 = (bf16[264,128]{1,0:T(8,128)(2,1)S(1)}, bf16[264,128]{1,0:T(8,128)(2,1)S(1)}, u32[]{:S(2)}, u32[]{:S(2)}) collective-permute-start(bf16[264,128]{1,0:T(8,128)(2,1)S(1)} %first_kernel.1.refs_0_), channel_id=1, source_target_pairs={{0,48},{8,56},{16,32},{24,40},{32,16},{40,24},{48,0},{56,8},{1,49}... | collective-permute-start | bytes 202760 | tf_op jit(solution)/shard_map/ppermute | solution.py:23
  13.2 0.0 copy-done.10
  13.2 0.1 subtract_dynamic-update-slice_fusion
  13.3 3.8 %collective-permute-done.1.refs_1_ = bf16[264,128]{1,0:T(8,128)(2,1)S(1)} collective-permute-done((bf16[264,128]{1,0:T(8,128)(2,1)S(1)}, bf16[264,128]{1,0:T(8,128)(2,1)S(1)}, u32[]{:S(2)}, u32[]{:S(2)}) %collective-permute-start.1) | collective-permute-done | bytes 67616 | tf_op jit(solution)/shard_map/ppermute | solution.py:23
  17.1 1.1 collective-permute-start.4
  18.2 1.7 %collective-permute-start.3 = (bf16[336,128]{1,0:T(8,128)(2,1)S(1)}, bf16[336,128]{1,0:T(8,128)(2,1)S(1)}, u32[]{:S(2)}, u32[]{:S(2)}) collective-permute-start(bf16[336,128]{1,0:T(8,128)(2,1)S(1)} %stage_kernel.2.refs_0_), channel_id=1, source_target_pairs={{0,16},{8,24},{16,0},{24,8},{32,48},{40,56},{48,32},{56,40},{1,17}... | collective-permute-start | bytes 258056 | tf_op jit(solution)/shard_map/ppermute | solution.py:23
  19.9 0.8 collective-permute-start.2
  20.7 0.1 convert_reduce_fusion
  20.8 4.7 %collective-permute-done.4.refs_3_ = bf16[336,128]{1,0:T(8,128)(2,1)S(1)} collective-permute-done((bf16[336,128]{1,0:T(8,128)(2,1)S(1)}, bf16[336,128]{1,0:T(8,128)(2,1)S(1)}, u32[]{:S(2)}, u32[]{:S(2)}) %collective-permute-start.4) | collective-permute-done | bytes 86048 | tf_op jit(solution)/shard_map/ppermute | solution.py:23
  25.4 0.0 collective-permute-done.3.refs_2_
  25.4 0.0 collective-permute-done.2.refs_1_
  25.5 2.8 %collective-permute-start.7 = (bf16[768,128]{1,0:T(8,128)(2,1)S(1)}, bf16[768,128]{1,0:T(8,128)(2,1)S(1)}, u32[]{:S(2)}, u32[]{:S(2)}) collective-permute-start(bf16[768,128]{1,0:T(8,128)(2,1)S(1)} %stage_kernel.3.refs_0_), channel_id=1, source_target_pairs={{0,6},{2,4},{4,2},{6,0},{1,7},{3,5},{5,3},{7,1},{8,14},{10,12},{12... | collective-permute-start | bytes 589832 | tf_op jit(solution)/shard_map/ppermute | solution.py:23
  28.3 0.8 collective-permute-start.6
  29.1 0.5 collective-permute-start.5
  29.7 0.7 reshape.29.vec_ref
  30.3 5.7 %collective-permute-done.7.refs_3_ = bf16[768,128]{1,0:T(8,128)(2,1)S(1)} collective-permute-done((bf16[768,128]{1,0:T(8,128)(2,1)S(1)}, bf16[768,128]{1,0:T(8,128)(2,1)S(1)}, u32[]{:S(2)}, u32[]{:S(2)}) %collective-permute-start.7) | collective-permute-done | bytes 196640 | tf_op jit(solution)/shard_map/ppermute | solution.py:23
  36.0 1.6 %collective-permute-done.6.refs_2_ = bf16[768,128]{1,0:T(8,128)(2,1)S(1)} collective-permute-done((bf16[768,128]{1,0:T(8,128)(2,1)S(1)}, bf16[768,128]{1,0:T(8,128)(2,1)S(1)}, u32[]{:S(2)}, u32[]{:S(2)}) %collective-permute-start.6) | collective-permute-done | bytes 196640 | tf_op jit(solution)/shard_map/ppermute | solution.py:23
  37.6 0.0 collective-permute-done.5.refs_1_
  37.6 3.1 %collective-permute-start.10 = (f32[96,128]{1,0:T(8,128)S(1)}, f32[96,128]{1,0:T(8,128)S(1)}, u32[]{:S(2)}, u32[]{:S(2)}) collective-permute-start(f32[96,128]{1,0:T(8,128)S(1)} %add_add_fusion.1), channel_id=1, source_target_pairs={{0,192},{64,128},{128,64},{192,0},{1,193},{65,129},{129,65},{193,1... | collective-permute-start | bytes 147464 | tf_op jit(solution)/shard_map/ppermute | solution.py:23
  40.7 0.6 collective-permute-start.9
  41.3 0.0 copy-done.2
  41.3 0.5 collective-permute-start.8
  41.8 0.9 copy-done.3
  42.8 0.0 copy-start.11
  42.8 0.0 copy-start.13
  42.8 3.1 %collective-permute-start.14 = (bf16[2304,128]{1,0:T(8,128)(2,1)S(1)}, bf16[2304,128]{1,0:T(8,128)(2,1)}, u32[]{:S(2)}, u32[]{:S(2)}) collective-permute-start(bf16[2304,128]{1,0:T(8,128)(2,1)S(1)} %join_kernel.1.base0), channel_id=1, source_target_pairs={{0,192},{64,128},{128,64},{192,0},{1,193},{65,129},{129,65},{193,1... | collective-permute-start | bytes 1769480 | tf_op jit(solution)/shard_map/ppermute | solution.py:23
  45.9 0.6 collective-permute-start.13
  46.5 0.0 collective-permute-done.10
  46.5 0.5 collective-permute-start.12
  47.0 0.0 collective-permute-done.9
  47.0 0.0 collective-permute-done.8
  47.0 0.1 collective-permute-start.11
  47.1 1.2 %collective-permute-done.11.other_ref = f32[96,128]{1,0:T(8,128)S(1)} collective-permute-done((f32[96,128]{1,0:T(8,128)S(1)}, f32[96,128]{1,0:T(8,128)S(1)}, u32[]{:S(2)}, u32[]{:S(2)}) %collective-permute-start.11) | collective-permute-done | bytes 49184 | tf_op jit(solution)/shard_map/ppermute | solution.py:23
  48.3 0.0 copy-done.7
  48.3 0.8 copy-done.4
  49.2 1.5 %column_sum.1 = (f32[4,32,192]{2,1,0:T(8,128)S(1)}, f32[32,15,128]{2,1,0:T(8,128)S(1)}) custom-call(f32[96,128]{1,0:T(8,128)S(1)} %add_add_fusion.own_ref, f32[96,128]{1,0:T(8,128)S(1)} %collective-permute-done.11.other_ref, f32[32,32]{1,0:T(8,128)S(1)} %copy-done.7, bf16[768,1536]{1,0:T(8,128)(2,1)S(1)} %copy-done, f32[32,3,128]{2,1,0:T(4,128)S(1)} %copy-done.4), custom_call_target="tpu_custom_call" | custom-call | tf_op jit(solution)/shard_map/column_sum/pallas_call | solution.py:203
  50.6 22.9 %all_to_all.10 = f32[32,15,128]{2,1,0:T(8,128)S(1)} all-to-all(f32[32,15,128]{2,1,0:T(8,128)S(1)} %get-tuple-element.34), channel_id=1, replica_groups=mesh['y'=4,'z'=8,'x'=4,'c'=2] {'z','x'}, dimensions={0} | all-to-all | bytes 491520 | tf_op jit(solution)/shard_map/all_to_all | solution.py:381
  73.6 0.0 collective-permute-done.14.base3
  73.6 0.0 collective-permute-done.13.base2
  73.6 0.0 collective-permute-done.12.base1
  73.6 3.1 %collective-permute-start.17 = (f32[15,128]{1,0:T(8,128)S(1)}, f32[15,128]{1,0:T(8,128)S(1)}, u32[]{:S(2)}, u32[]{:S(2)}) collective-permute-start(f32[15,128]{1,0:T(8,128)S(1)} %reduce_sum.9), channel_id=1, source_target_pairs={{0,192},{64,128},{128,64},{192,0},{1,193},{65,129},{129,65},{193,1... | collective-permute-start | bytes 23048 | tf_op jit(solution)/shard_map/ppermute | solution.py:23
  76.7 0.6 collective-permute-start.16
  77.3 0.5 collective-permute-start.15
  77.8 0.8 collective-permute-done.17
  78.6 3.2 %collective-permute-done.16 = f32[15,128]{1,0:T(8,128)S(1)} collective-permute-done((f32[15,128]{1,0:T(8,128)S(1)}, f32[15,128]{1,0:T(8,128)S(1)}, u32[]{:S(2)}, u32[]{:S(2)}) %collective-permute-start.16) | collective-permute-done | bytes 7712 | tf_op jit(solution)/shard_map/ppermute | solution.py:23
  81.9 0.0 collective-permute-done.15
  81.9 0.7 broadcast_in_dim.13
  82.6 7.4 %all-to-all-start.1 = ((f32[32,15,128]{2,1,0:T(8,128)}), f32[32,15,128]{2,1,0:T(8,128)S(1)}, u32[]{:S(2)}, u32[]{:S(2)}) async-start(f32[32,15,128]{2,1,0:T(8,128)} %broadcast_in_dim.13), calls=%async_computation.1 | async-start | bytes 524288 | tf_op jit(solution)/shard_map/all_to_all | solution.py:385
  90.0 0.6 pad_add_fusion.where
  90.6 0.7 dynamic-slice_bitcast_fusion.own_basis_ref
  91.2 9.5 %all-to-all-done.1.piece_ref = f32[32,15,128]{2,1,0:T(8,128)S(1)} async-done(((f32[32,15,128]{2,1,0:T(8,128)}), f32[32,15,128]{2,1,0:T(8,128)S(1)}, u32[]{:S(2)}, u32[]{:S(2)}) %all-to-all-start.1) | async-done | bytes 245792 | tf_op jit(solution)/shard_map/all_to_all | solution.py:385
  100.8 0.7 convert_element_type.49
  101.5 0.0 copy-done.11
  101.5 0.6 multiply_subtract_fusion
  102.1 0.0 copy-done.1
  102.1 7.5 %apply.1 = (bf16[768,1536]{1,0:T(8,128)(2,1)}, bf16[768,1536]{1,0:T(8,128)(2,1)}, f32[6,1536]{1,0:T(8,128)}, f32[6,1536]{1,0:T(8,128)}) custom-call(s32[3]{0:T(128)} %pad_add_fusion.where, f32[32,6]{1,0:T(8,128)} %dynamic-slice_bitcast_fusion.own_basis_ref, f32[32,15,128]{2,1,0:T(8,128)} %copy-done.8, bf16[768,1536]{1,0:T(8,128)(2,1)} %get-tuple-element.31.merged_ref, ...), custom_call_target="tpu_custom_call" | custom-call | tf_op jit(solution)/shard_map/apply/pallas_call | solution.py:295
  (26 shorter events, 0.3 us)
Async XLA Ops:
  0.6 12.6 %copy-start.10 = (f32[42]{0:T(128)S(1)}, f32[42]{0:T(128)}, u32[]{:S(2)}) copy-start(f32[42]{0:T(128)} %param.16) | copy-start | bytes 508
  0.6 12.6 %copy-start.12 = (f32[42]{0:T(128)S(1)}, f32[42]{0:T(128)}, u32[]{:S(2)}) copy-start(f32[42]{0:T(128)} %param.17) | copy-start | bytes 508
  0.7 20.1 %copy-start.9 = (bf16[1,5376]{1,0:T(2,128)(2,1)S(1)}, bf16[1,5376]{1,0:T(2,128)(2,1)}, u32[]{:S(2)}) copy-start(bf16[1,5376]{1,0:T(2,128)(2,1)} %param.15) | copy-start | bytes 32260
  0.7 47.6 %copy-start.7 = (f32[32,32]{1,0:T(8,128)S(1)}, f32[32,32]{1,0:T(8,128)}, u32[]{:S(2)}) copy-start(f32[32,32]{1,0:T(8,128)} %gram_ref.1) | copy-start | bytes 12292
  5.3 43.0 %copy-start = (bf16[768,1536]{1,0:T(8,128)(2,1)S(1)}, bf16[768,1536]{1,0:T(8,128)(2,1)}, u32[]{:S(2)}) copy-start(bf16[768,1536]{1,0:T(8,128)(2,1)} %get-tuple-element.31.merged_ref) | copy-start | bytes 7077892
  5.3 1.5 %collective-permute-start = (f32[96,128]{1,0:T(8,128)}, f32[96,128]{1,0:T(8,128)S(1)}, u32[]{:S(2)}, u32[]{:S(2)}) collective-permute-start(f32[96,128]{1,0:T(8,128)} %get-tuple-element.27), channel_id=1, source_target_pairs={{0,1},{1,0},{2,3},{3,2},{4,5},{5,4},{6,7},{7,6},{8,9},{9,8},{10,11... | collective-permute-start | bytes 147464 | tf_op jit(solution)/shard_map/ppermute | solution.py:354
  6.8 0.9 copy-start.6
  7.7 9.4 %collective-permute-start.1 = (bf16[264,128]{1,0:T(8,128)(2,1)S(1)}, bf16[264,128]{1,0:T(8,128)(2,1)S(1)}, u32[]{:S(2)}, u32[]{:S(2)}) collective-permute-start(bf16[264,128]{1,0:T(8,128)(2,1)S(1)} %first_kernel.1.refs_0_), channel_id=1, source_target_pairs={{0,48},{8,56},{16,32},{24,40},{32,16},{40,24},{48,0},{56,8},{1,49}... | collective-permute-start | bytes 202760 | tf_op jit(solution)/shard_map/ppermute | solution.py:23
  17.1 8.3 %collective-permute-start.4 = (bf16[336,128]{1,0:T(8,128)(2,1)S(1)}, bf16[336,128]{1,0:T(8,128)(2,1)S(1)}, u32[]{:S(2)}, u32[]{:S(2)}) collective-permute-start(bf16[336,128]{1,0:T(8,128)(2,1)S(1)} %stage_kernel.2.refs_0_), channel_id=1, source_target_pairs={{0,24},{8,16},{16,8},{24,0},{32,56},{40,48},{48,40},{56,32},{1,25}... | collective-permute-start | bytes 258056 | tf_op jit(solution)/shard_map/ppermute | solution.py:23
  18.2 7.2 %collective-permute-start.3 = (bf16[336,128]{1,0:T(8,128)(2,1)S(1)}, bf16[336,128]{1,0:T(8,128)(2,1)S(1)}, u32[]{:S(2)}, u32[]{:S(2)}) collective-permute-start(bf16[336,128]{1,0:T(8,128)(2,1)S(1)} %stage_kernel.2.refs_0_), channel_id=1, source_target_pairs={{0,16},{8,24},{16,0},{24,8},{32,48},{40,56},{48,32},{56,40},{1,17}... | collective-permute-start | bytes 258056 | tf_op jit(solution)/shard_map/ppermute | solution.py:23
  19.9 5.5 %collective-permute-start.2 = (bf16[336,128]{1,0:T(8,128)(2,1)S(1)}, bf16[336,128]{1,0:T(8,128)(2,1)S(1)}, u32[]{:S(2)}, u32[]{:S(2)}) collective-permute-start(bf16[336,128]{1,0:T(8,128)(2,1)S(1)} %stage_kernel.2.refs_0_), channel_id=1, source_target_pairs={{0,8},{8,0},{16,24},{24,16},{32,40},{40,32},{48,56},{56,48},{1,9},... | collective-permute-start | bytes 258056 | tf_op jit(solution)/shard_map/ppermute | solution.py:23
  25.5 10.5 %collective-permute-start.7 = (bf16[768,128]{1,0:T(8,128)(2,1)S(1)}, bf16[768,128]{1,0:T(8,128)(2,1)S(1)}, u32[]{:S(2)}, u32[]{:S(2)}) collective-permute-start(bf16[768,128]{1,0:T(8,128)(2,1)S(1)} %stage_kernel.3.refs_0_), channel_id=1, source_target_pairs={{0,6},{2,4},{4,2},{6,0},{1,7},{3,5},{5,3},{7,1},{8,14},{10,12},{12... | collective-permute-start | bytes 589832 | tf_op jit(solution)/shard_map/ppermute | solution.py:23
  28.3 9.2 %collective-permute-start.6 = (bf16[768,128]{1,0:T(8,128)(2,1)S(1)}, bf16[768,128]{1,0:T(8,128)(2,1)S(1)}, u32[]{:S(2)}, u32[]{:S(2)}) collective-permute-start(bf16[768,128]{1,0:T(8,128)(2,1)S(1)} %stage_kernel.3.refs_0_), channel_id=1, source_target_pairs={{0,4},{2,6},{4,0},{6,2},{1,5},{3,7},{5,1},{7,3},{8,12},{10,14},{12... | collective-permute-start | bytes 589832 | tf_op jit(solution)/shard_map/ppermute | solution.py:23
  29.1 8.4 %collective-permute-start.5 = (bf16[768,128]{1,0:T(8,128)(2,1)S(1)}, bf16[768,128]{1,0:T(8,128)(2,1)S(1)}, u32[]{:S(2)}, u32[]{:S(2)}) collective-permute-start(bf16[768,128]{1,0:T(8,128)(2,1)S(1)} %stage_kernel.3.refs_0_), channel_id=1, source_target_pairs={{0,2},{2,0},{4,6},{6,4},{1,3},{3,1},{5,7},{7,5},{8,10},{10,8},{12,... | collective-permute-start | bytes 589832 | tf_op jit(solution)/shard_map/ppermute | solution.py:23
  37.6 3.8 %copy-start.2 = (bf16[768,128]{1,0:T(8,128)(2,1)}, bf16[768,128]{1,0:T(8,128)(2,1)S(1)}, u32[]{:S(2)}) copy-start(bf16[768,128]{1,0:T(8,128)(2,1)S(1)} %collective-permute-done.5.refs_1_) | copy-start | bytes 589828
  37.6 8.9 %collective-permute-start.10 = (f32[96,128]{1,0:T(8,128)S(1)}, f32[96,128]{1,0:T(8,128)S(1)}, u32[]{:S(2)}, u32[]{:S(2)}) collective-permute-start(f32[96,128]{1,0:T(8,128)S(1)} %add_add_fusion.1), channel_id=1, source_target_pairs={{0,192},{64,128},{128,64},{192,0},{1,193},{65,129},{129,65},{193,1... | collective-permute-start | bytes 147464 | tf_op jit(solution)/shard_map/ppermute | solution.py:23
  40.7 6.3 %collective-permute-start.9 = (f32[96,128]{1,0:T(8,128)S(1)}, f32[96,128]{1,0:T(8,128)S(1)}, u32[]{:S(2)}, u32[]{:S(2)}) collective-permute-start(f32[96,128]{1,0:T(8,128)S(1)} %add_add_fusion.1), channel_id=1, source_target_pairs={{0,128},{64,192},{128,0},{192,64},{1,129},{65,193},{129,1},{193,65... | collective-permute-start | bytes 147464 | tf_op jit(solution)/shard_map/ppermute | solution.py:23
  41.3 5.6 %collective-permute-start.8 = (f32[96,128]{1,0:T(8,128)S(1)}, f32[96,128]{1,0:T(8,128)S(1)}, u32[]{:S(2)}, u32[]{:S(2)}) collective-permute-start(f32[96,128]{1,0:T(8,128)S(1)} %add_add_fusion.1), channel_id=1, source_target_pairs={{0,64},{64,0},{128,192},{192,128},{1,65},{65,1},{129,193},{193,129... | collective-permute-start | bytes 147464 | tf_op jit(solution)/shard_map/ppermute | solution.py:23
  41.8 0.9 copy-start.3
  42.7 59.3 %copy-start.1 = (bf16[2304,128]{1,0:T(8,128)(2,1)}, bf16[2304,128]{1,0:T(8,128)(2,1)S(1)}, u32[]{:S(2)}) copy-start(bf16[2304,128]{1,0:T(8,128)(2,1)S(1)} %join_kernel.1.base0) | copy-start | bytes 1769476
  42.8 58.7 %copy-start.11 = (f32[42]{0:T(128)S(1)}, f32[42]{0:T(128)}, u32[]{:S(2)}) copy-start(f32[42]{0:T(128)} %param.16) | copy-start | bytes 508
  42.8 58.7 %copy-start.13 = (f32[42]{0:T(128)S(1)}, f32[42]{0:T(128)}, u32[]{:S(2)}) copy-start(f32[42]{0:T(128)} %param.17) | copy-start | bytes 508
  42.8 30.8 %collective-permute-start.14 = (bf16[2304,128]{1,0:T(8,128)(2,1)S(1)}, bf16[2304,128]{1,0:T(8,128)(2,1)}, u32[]{:S(2)}, u32[]{:S(2)}) collective-permute-start(bf16[2304,128]{1,0:T(8,128)(2,1)S(1)} %join_kernel.1.base0), channel_id=1, source_target_pairs={{0,192},{64,128},{128,64},{192,0},{1,193},{65,129},{129,65},{193,1... | collective-permute-start | bytes 1769480 | tf_op jit(solution)/shard_map/ppermute | solution.py:23
  45.9 27.7 %collective-permute-start.13 = (bf16[2304,128]{1,0:T(8,128)(2,1)S(1)}, bf16[2304,128]{1,0:T(8,128)(2,1)}, u32[]{:S(2)}, u32[]{:S(2)}) collective-permute-start(bf16[2304,128]{1,0:T(8,128)(2,1)S(1)} %join_kernel.1.base0), channel_id=1, source_target_pairs={{0,128},{64,192},{128,0},{192,64},{1,129},{65,193},{129,1},{193,65... | collective-permute-start | bytes 1769480 | tf_op jit(solution)/shard_map/ppermute | solution.py:23
  46.5 27.1 %collective-permute-start.12 = (bf16[2304,128]{1,0:T(8,128)(2,1)S(1)}, bf16[2304,128]{1,0:T(8,128)(2,1)}, u32[]{:S(2)}, u32[]{:S(2)}) collective-permute-start(bf16[2304,128]{1,0:T(8,128)(2,1)S(1)} %join_kernel.1.base0), channel_id=1, source_target_pairs={{0,64},{64,0},{128,192},{192,128},{1,65},{65,1},{129,193},{193,129... | collective-permute-start | bytes 1769480 | tf_op jit(solution)/shard_map/ppermute | solution.py:23
  47.0 1.3 %collective-permute-start.11 = (f32[96,128]{1,0:T(8,128)S(1)}, f32[96,128]{1,0:T(8,128)S(1)}, u32[]{:S(2)}, u32[]{:S(2)}) collective-permute-start(f32[96,128]{1,0:T(8,128)S(1)} %add_add_fusion.own_ref), channel_id=1, source_target_pairs={{0,1},{1,0},{2,3},{3,2},{4,5},{5,4},{6,7},{7,6},{8,9},{9,8},{10,11... | collective-permute-start | bytes 147464 | tf_op jit(solution)/shard_map/ppermute | solution.py:23
  48.3 0.8 copy-start.4
  50.6 51.5 %copy-start.5 = (f32[4,32,192]{2,1,0:T(8,128)}, f32[4,32,192]{2,1,0:T(8,128)S(1)}, u32[]{:S(2)}) copy-start(f32[4,32,192]{2,1,0:T(8,128)S(1)} %get-tuple-element.33.basis_hbm) | copy-start | bytes 294916
  73.6 5.0 %collective-permute-start.17 = (f32[15,128]{1,0:T(8,128)S(1)}, f32[15,128]{1,0:T(8,128)S(1)}, u32[]{:S(2)}, u32[]{:S(2)}) collective-permute-start(f32[15,128]{1,0:T(8,128)S(1)} %reduce_sum.9), channel_id=1, source_target_pairs={{0,192},{64,128},{128,64},{192,0},{1,193},{65,129},{129,65},{193,1... | collective-permute-start | bytes 23048 | tf_op jit(solution)/shard_map/ppermute | solution.py:23
  76.7 5.2 %collective-permute-start.16 = (f32[15,128]{1,0:T(8,128)S(1)}, f32[15,128]{1,0:T(8,128)S(1)}, u32[]{:S(2)}, u32[]{:S(2)}) collective-permute-start(f32[15,128]{1,0:T(8,128)S(1)} %reduce_sum.9), channel_id=1, source_target_pairs={{0,128},{64,192},{128,0},{192,64},{1,129},{65,193},{129,1},{193,65... | collective-permute-start | bytes 23048 | tf_op jit(solution)/shard_map/ppermute | solution.py:23
  77.3 4.5 %collective-permute-start.15 = (f32[15,128]{1,0:T(8,128)S(1)}, f32[15,128]{1,0:T(8,128)S(1)}, u32[]{:S(2)}, u32[]{:S(2)}) collective-permute-start(f32[15,128]{1,0:T(8,128)S(1)} %reduce_sum.9), channel_id=1, source_target_pairs={{0,64},{64,0},{128,192},{192,128},{1,65},{65,1},{129,193},{193,129... | collective-permute-start | bytes 23048 | tf_op jit(solution)/shard_map/ppermute | solution.py:23
  82.6 18.2 %all-to-all-start.1 = ((f32[32,15,128]{2,1,0:T(8,128)}), f32[32,15,128]{2,1,0:T(8,128)S(1)}, u32[]{:S(2)}, u32[]{:S(2)}) async-start(f32[32,15,128]{2,1,0:T(8,128)} %broadcast_in_dim.13), calls=%async_computation.1 | async-start | bytes 524288 | tf_op jit(solution)/shard_map/all_to_all | solution.py:385
  100.8 1.3 %copy-start.8 = (f32[32,15,128]{2,1,0:T(8,128)}, f32[32,15,128]{2,1,0:T(8,128)S(1)}, u32[]{:S(2)}) copy-start(f32[32,15,128]{2,1,0:T(8,128)S(1)} %all-to-all-done.1.piece_ref) | copy-start | bytes 737284

commit v4 on v3

--- a/solution.py
+++ b/solution.py
@@ -140,6 +140,20 @@
         out_ref[first : first + n, :] = b[2 * n_sums :, :]
 
 
+def halves_kernel(n_sums, *refs):
+    *blocks, out_ref, rest_ref = refs
+    high, low = split(total([sums_of(b[: 2 * n_sums, :], n_sums) for b in blocks]))
+    out_ref[:n_sums, :] = high
+    out_ref[n_sums : 2 * n_sums, :] = low
+    n = blocks[0].shape[0] - 2 * n_sums
+    half = len(blocks) // 2
+    for j, b in enumerate(blocks[:half]):
+        first = 2 * n_sums + j * n
+        out_ref[first : first + n, :] = b[2 * n_sums :, :]
+    for j, b in enumerate(blocks[half:]):
+        rest_ref[j * n : (j + 1) * n, :] = b[2 * n_sums :, :]
+
+
 def join_kernel(n_sums, *refs):
     *blocks, out_ref = refs
     n = blocks[0].shape[0] - 2 * n_sums
@@ -156,9 +170,24 @@
     )(*blocks)
 
 
+def repeat_kernel(*refs):
+    *blocks, out_ref = refs
+    out_ref[...] = jnp.broadcast_to(total([b[...] for b in blocks])[None], out_ref.shape)
+
+
+def repeat_call(blocks, n):
+    return pl.pallas_call(
+        repeat_kernel,
+        out_shape=jax.ShapeDtypeStruct((n, *blocks[0].shape), jnp.float32),
+        compiler_params=pltpu.CompilerParams(vmem_limit_bytes=8 << 20),
+        name="repeat",
+    )(*blocks)
+
+
 def column_kernel(own_ref, other_ref, gram_ref, merged_ref, vec_ref, basis_ref, piece_ref, basis_b):
     step = pl.program_id(0)
     groups = merged_ref.shape[1] // LANES
+    n_vec = vec_ref.shape[0] // gram_ref.shape[0]
     half = own_ref.shape[0] // (basis_b.shape[1] // LANES)
 
     @pl.when(step == 0)
@@ -181,11 +210,12 @@
         for k in range(basis_ref.shape[0]):
             basis_ref[k] = basis[:, k * width : (k + 1) * width]
         basis_b[...] = basis.astype(jnp.bfloat16)
-        n_vec = vec_ref.shape[1]
-        piece_ref[:, piece_ref.shape[1] - n_vec :, :] = vec_ref[...]
+        rank = gram_ref.shape[0]
+        for k in range(n_vec):
+            piece_ref[:, piece_ref.shape[1] - n_vec + k, :] = vec_ref[k * rank : (k + 1) * rank, :]
 
     part = jnp.dot(basis_b[...], merged_ref[...], preferred_element_type=jnp.float32)
-    for j in range(pl.cdiv(piece_ref.shape[1] - vec_ref.shape[1], groups)):
+    for j in range(pl.cdiv(piece_ref.shape[1] - n_vec, groups)):
 
         @pl.when(step == j)
         def _():
@@ -197,7 +227,7 @@
     rank = gram_inverse.shape[0]
     rows, cols = merged.shape
     block = 512
-    pieces = cols // LANES + vec.shape[1]
+    pieces = cols // LANES + vec.shape[0] // rank
     basis_shape = (SIZES["y"], rank, rows // SIZES["y"])
     whole = lambda *shape: pl.BlockSpec(shape, lambda j: (0,) * len(shape))
     return pl.pallas_call(
@@ -235,18 +265,26 @@
 
 
 def apply_kernel(
-    where, own_basis_ref, piece_ref, merged_ref, basis_hbm, base0, base1, base2, base3, master_hbm, momentum_hbm,
-    new_error_ref, weights_ref, new_master_ref, new_momentum_ref,
-    cols3, lane_rows, basis, base_blocks, master, momentum, sems,
+    where, own_basis_ref, piece_ref, merged_ref, basis_hbm, base0, base1, base2, base3,
+    rest0, rest1, rest2, rest3, master_hbm, momentum_hbm,
+    vec_master_ref, vec_momentum_ref,
+    new_error_ref, weights_ref, new_master_ref, new_momentum_ref, vec_weights_ref, vec_new_master_ref, vec_new_momentum_ref,
+    cols3, lane_rows, basis, base_blocks, master, momentum, vec, sems,
 ):
     step = pl.program_id(0)
     cols = merged_ref.shape[1]
     groups = cols // LANES
     nx, ny, nz = SIZES["x"], SIZES["y"], SIZES["z"]
-    shard = base0.shape[0] // (nx * nz)
-    sources = (basis_hbm, base0, base1, base2, base3, master_hbm, momentum_hbm)
-    targets = (basis, *[base_blocks.at[k] for k in range(ny)], master, momentum)
-    copies = [pltpu.make_async_copy(s, t, sems.at[k]) for k, (s, t) in enumerate(zip(sources, targets))]
+    half = base0.shape[0]
+    shard = half // (nx * nz // 2)
+    part = half // nx
+    moves = [(basis_hbm, basis)]
+    for k, base in enumerate((base0, base1, base2, base3)):
+        moves.append((base, base_blocks.at[k, pl.ds(0, half)]))
+        for j, rest in enumerate((rest0, rest1, rest2, rest3)):
+            moves.append((rest.at[pl.ds(k * part, part)], base_blocks.at[k, pl.ds(half + j * part, part)]))
+    moves += [(master_hbm, master), (momentum_hbm, momentum)]
+    copies = [pltpu.make_async_copy(s, t, sems.at[k]) for k, (s, t) in enumerate(moves)]
 
     @pl.when(step == 0)
     def _():
@@ -261,11 +299,12 @@
 
         @pl.when(step == k)
         def _():
-            copies[1 + k].wait()
+            for copy in copies[1 + k * (nx + 1) : 1 + (k + 1) * (nx + 1)]:
+                copy.wait()
             for j in range(nx):
                 for d in range(nz):
                     place = (where[1] ^ (d // 2) ^ (d % 2 * 6)) * nx + (where[2] ^ j)
-                    source = (j * nz + d) * shard
+                    source = d // (nz // 2) * half + (j * (nz // 2) + d % (nz // 2)) * shard
                     lane_rows[pl.ds(pl.multiple_of(place * shard, 8), shard), :] = base_blocks[
                         k, source : source + shard, :
                     ].astype(jnp.float32)
@@ -286,8 +325,27 @@
         new_momentum_ref[...] = new
         new_master_ref[...] = master[...] - step_size * (rows_approx + momentum_decay * new)
 
-
-def apply_call(where, row_basis, own_basis, pieces, merged, bases, master, momentum):
+        rank = piece_ref.shape[0]
+        for k in range(piece_ref.shape[1] - groups):
+            vec[k * rank : (k + 1) * rank, :] = piece_ref[:, groups + k, :]
+        n_vec = vec_weights_ref.shape[0]
+        change = gain * (vec[:n_vec, :] / REPLICAS)
+        vec_weights_ref[...] = (vec[n_vec : 2 * n_vec, :] - change).astype(jnp.bfloat16)
+        shard_len = vec_master_ref.shape[1]
+        start = ((where[0] * nz + where[1]) * nx + where[2]) * shard_len
+        row, lane = start // LANES, start % LANES
+        turned = [
+            pltpu.roll(jnp.broadcast_to(vec[pl.ds(row + k, 1), :], (8, LANES)), LANES - lane, 1)
+            for k in range(2)
+        ]
+        here = lax.broadcasted_iota(jnp.int32, (8, LANES), 1) < LANES - lane
+        mean = jnp.where(here, turned[0], turned[1])[:1, :shard_len] / REPLICAS
+        new = momentum_decay * vec_momentum_ref[...] + mean
+        vec_new_momentum_ref[...] = new
+        vec_new_master_ref[...] = vec_master_ref[...] - step_size * (mean + momentum_decay * new)
+
+
+def apply_call(where, row_basis, own_basis, pieces, merged, bases, master, momentum, vec_len, vec_master, vec_momentum):
     _, rank, block = row_basis.shape
     rows, cols = merged.shape
     spec = pl.BlockSpec((block, cols), lambda i, s: (s[0] ^ i, 0))
@@ -297,16 +355,22 @@
         grid_spec=pltpu.PrefetchScalarGridSpec(
             num_scalar_prefetch=1,
             grid=(SIZES["y"],),
-            in_specs=[whole(own_basis), whole(pieces), spec, *[HBM] * (3 + len(bases))],
-            out_specs=[spec, spec, whole(master), whole(momentum)],
+            in_specs=[
+                whole(own_basis), whole(pieces), spec, *[HBM] * (3 + len(bases)), whole(vec_master), whole(vec_master),
+            ],
+            out_specs=[
+                spec, spec, whole(master), whole(momentum),
+                pl.BlockSpec((vec_len // LANES, LANES), lambda i, s: (0, 0)), whole(vec_master), whole(vec_master),
+            ],
             scratch_shapes=[
                 pltpu.VMEM((6 * rank, cols), jnp.bfloat16),
-                pltpu.VMEM(bases[0].shape, jnp.float32),
+                pltpu.VMEM((2 * bases[0].shape[0], LANES), jnp.float32),
                 pltpu.VMEM(row_basis.shape, jnp.float32),
-                pltpu.VMEM((len(bases), *bases[0].shape), jnp.bfloat16),
+                pltpu.VMEM((SIZES["y"], 2 * bases[0].shape[0], LANES), jnp.bfloat16),
                 pltpu.VMEM(master.shape, jnp.float32),
                 pltpu.VMEM(master.shape, jnp.float32),
-                pltpu.SemaphoreType.DMA((3 + len(bases),)),
+                pltpu.VMEM((rank * (pieces.shape[1] - cols // LANES), LANES), jnp.float32),
+                pltpu.SemaphoreType.DMA((3 + SIZES["y"] * (SIZES["x"] + 1),)),
             ],
         ),
         out_shape=[
@@ -314,10 +378,13 @@
             jax.ShapeDtypeStruct((rows, cols), jnp.bfloat16),
             jax.ShapeDtypeStruct(master.shape, jnp.float32),
             jax.ShapeDtypeStruct(master.shape, jnp.float32),
+            jax.ShapeDtypeStruct((vec_len // LANES, LANES), jnp.bfloat16),
+            jax.ShapeDtypeStruct(vec_master.shape, jnp.float32),
+            jax.ShapeDtypeStruct(vec_master.shape, jnp.float32),
         ],
         compiler_params=pltpu.CompilerParams(vmem_limit_bytes=60 << 20),
         name="apply",
-    )(where, own_basis, pieces, merged, row_basis, *bases, master, momentum)
+    )(where, own_basis, pieces, merged, row_basis, *bases, master, momentum, vec_master, vec_momentum)
 
 
 def vec_rows_of(rank, replica_index, vec_grads, vec_master, vec_momentum):
@@ -330,7 +397,7 @@
     vec = jnp.concatenate([vec_grads[0].astype(jnp.float32), vec_base], 0)
     vec_rows = pl.cdiv(vec.shape[0], rank * LANES)
     vec = jnp.pad(vec, (0, vec_rows * rank * LANES - vec.shape[0]))
-    return vec.reshape(rank, vec_rows, LANES)
+    return vec.reshape(vec_rows * rank, LANES)
 
 
 def on_device(
@@ -358,52 +425,49 @@
     blocks = flips(payload, "z", (0, 6))
     payload = blocks_call(stage_kernel, blocks, n_sums, lanes(2 * n_sums + 2 * n_base))
     blocks = flips(payload, "z", (0, 1, 2, 3))
-    payload = blocks_call(stage_kernel, blocks, n_sums, lanes(2 * n_sums + 8 * n_base))
+    payload, rest = blocks_call(
+        halves_kernel, blocks, n_sums, [lanes(2 * n_sums + 4 * n_base), lanes(4 * n_base)]
+    )
     blocks = flips(payload, "x")
+    rests = flips(rest, "y")
     sums = total([sums_of(b, n_sums) for b in blocks])
-    base = blocks_call(join_kernel, blocks, n_sums, lanes(32 * n_base))
+    base = blocks_call(join_kernel, blocks, n_sums, lanes(16 * n_base))
+    rest = blocks_call(join_kernel, rests, 0, lanes(16 * n_base))
     vec = vec_rows_of(rank, replica_index, vec_grads, vec_master, vec_momentum)
     sums, vec = lax.optimization_barrier((sums, vec))
     sums = total(flips(sums, "y"))
-    bases = flips(base, "y")
+    bases = flips(base, "y") + flips(rest, "x")
     own, other = flips(sums, "c")
-    own, other, bases[0] = lax.optimization_barrier((own, other, bases[0]))
-
-    vec_len = vec_grads.shape[1]
-    shard_len = vec_master.shape[0]
-    vec_rows = vec.shape[1]
+    own, other, bases[0], bases[4] = lax.optimization_barrier((own, other, bases[0], bases[4]))
+
     row_basis, pieces = column_call(own, other, gram_inverse, merged, vec)
     state_rows = fc_master.shape[0]
     own_basis = lax.dynamic_slice(
         row_basis, (y, 0, (z * SIZES["x"] + x) * state_rows), (1, rank, state_rows)
     )[0]
 
+    near = (1, 5)
+    pieces, *arrived = lax.optimization_barrier((pieces, *[bases[k] for k in near]))
+    for k, block in zip(near, arrived):
+        bases[k] = block
     pieces = lax.all_to_all(pieces, ("z", "x"), 0, 0, tiled=True)
     piece, *bases = lax.optimization_barrier((jnp.sum(pieces, 0), *bases))
-    piece = total(flips(piece, "y"))
-    pieces = jnp.broadcast_to(piece[None], (rank,) + piece.shape)
+    pieces = repeat_call(flips(piece, "y"), rank)
     pieces = lax.all_to_all(pieces, ("z", "x"), 0, 0, tiled=True)
 
     where = jnp.stack([y, z, x]).astype(jnp.int32)
-    new_error, new_weights, new_master, new_momentum = apply_call(
-        where, row_basis, own_basis, pieces, merged, bases, fc_master, fc_momentum
+    new_error, new_weights, new_master, new_momentum, vec_weights, vec_new_master, vec_new_momentum = apply_call(
+        where, row_basis, own_basis, pieces, merged, bases, fc_master, fc_momentum,
+        vec_grads.shape[1], vec_master[None], vec_momentum[None],
     )
-
-    vec = pieces[:, -vec_rows:].reshape(-1)
-    vec_total = vec[:vec_len] / REPLICAS
-    vec_base = vec[vec_len : 2 * vec_len]
-    vec_mean = lax.dynamic_slice_in_dim(vec_total, replica_index * shard_len, shard_len, 0)
-    vec_new_momentum = momentum_decay * vec_momentum + vec_mean
-    vec_new_master = vec_master - step_size * (vec_mean + momentum_decay * vec_new_momentum)
-    vec_weights = (vec_base - gain * vec_total).astype(jnp.bfloat16)
     return (
         new_error[None],
         new_momentum,
         new_master,
         new_weights,
-        vec_new_momentum,
-        vec_new_master,
-        vec_weights,
+        vec_new_momentum[0],
+        vec_new_master[0],
+        vec_weights.reshape(-1),
     )
 
 

time: 110 us -> 115 us (1.045)
  blocking collectives: 22.9 us -> 0 us
  starting transfers between devices: 33.3 us -> 55.6 us
  waiting for transfers between devices: 31.9 us -> 38.6 us
  local copies, waits for them, and re-layouts: 5.43 us -> 3.04 us
  Pallas kernels: 13.6 us -> 15.2 us
    all_to_all x1 -> x0, blocking collectives: 22.9 us -> none  [on_device(): pieces = lax.all_to_all(pieces, ('z', 'x'), 0, 0, tiled=True)]
    all_to_all x1 -> x2, starting transfers between devices: 7.36 us -> 19.8 us  [on_device(): pieces = lax.all_to_all(pieces, ('z', 'x'), 0, 0, tiled=True)]
    ppermute x17 -> x23, starting transfers between devices: 25.9 us -> 35.7 us  [flips(): lax.ppermute(value, axis, [(i, i ^ d) for i in range(n)])]
    all_to_all x1 -> x2, waiting for transfers between devices: 9.52 us -> 14.6 us  [on_device(): pieces = lax.all_to_all(pieces, ('z', 'x'), 0, 0, tiled=True)]
    ppermute x17 -> x23, waiting for transfers between devices: 21 us -> 22.6 us  [flips(): lax.ppermute(value, axis, [(i, i ^ d) for i in range(n)])]
    unnamed x28 -> x32, local copies, waits for them, and re-layouts: 2.71 us -> 2.35 us
  transfers between devices with their start and end apart: 19 -> 26, of which waited for: 9 -> 12; matrix products, arithmetic and copies ran while one was open for 2% -> 1% of each run, Pallas kernels for 1% -> 2%
where the time goes in v4:
time: 115 us; the launch traced here: 114 us
  starting transfers between devices  55.6 us (48%)
  waiting for transfers between devices  38.6 us (34%)
  Pallas kernels  15.2 us (13%)
  local copies, waits for them, and re-layouts  3.04 us (3%)
    ppermute x23, starting transfers between devices, flips(): lax.ppermute(value, axis, [(i, i ^ d) for i in range(n)])  35.7 us
    ppermute x23, waiting for transfers between devices, flips(): lax.ppermute(value, axis, [(i, i ^ d) for i in range(n)])  22.6 us
    all_to_all x2, starting transfers between devices, on_device(): pieces = lax.all_to_all(pieces, ('z', 'x'), 0, 0, tiled=True)  19.8 us
    all_to_all x2, waiting for transfers between devices, on_device(): pieces = lax.all_to_all(pieces, ('z', 'x'), 0, 0, tiled=True)  14.6 us
    pallas_call x1, Pallas kernels, apply_call(): pl.pallas_call(apply_kernel, grid_spec=pltpu.PrefetchScalarGridSpec(num_s...  7.62 us
    pallas_call x1, Pallas kernels, row_call(): pl.pallas_call(row_kernel, in_specs=[HBM] * 5, out_specs=[HBM] + [pl.Bloc...  4.6 us
    unnamed x32, local copies, waits for them, and re-layouts  2.35 us
  transfers between devices with their start and end apart: 26, of which 12 were waited for; matrix products, arithmetic and copies ran while one was open for 1% of the time, Pallas kernels for 2%

profile of v4, /device:TPU:32, one launch (start us, length us, event | category | flops | bytes accessed | tf_op | source)
XLA Modules:
  0.0 114.4 jit_solution(6964537490680793520)
XLA Ops:
  0.6 0.0 copy-start.14
  0.6 0.0 copy-start.15
  0.7 4.6 %row_sum.1 = (bf16[768,1536]{1,0:T(8,128)(2,1)}, f32[168,128]{1,0:T(8,128)}, f32[96,128]{1,0:T(8,128)}) custom-call(f32[32,1536]{1,0:T(8,128)} %bitcast.18, bf16[768,1536]{1,0:T(8,128)(2,1)} %bitcast.16, bf16[768,1536]{1,0:T(8,128)(2,1)} %bitcast.17, f32[6,1536]{1,0:T(8,128)} %master_hbm.3, f32[6,1536]{1,0:T(8,128)} %momentum_hbm.3), custom_call_target="tpu_custom_call" | custom-call | tf_op jit(solution)/shard_map/row_sum/pallas_call | solution.py:92
  5.3 0.1 collective-permute-start
  5.4 1.4 %collective-permute-done.other_ref = f32[96,128]{1,0:T(8,128)S(1)} collective-permute-done((f32[96,128]{1,0:T(8,128)}, f32[96,128]{1,0:T(8,128)S(1)}, u32[]{:S(2)}, u32[]{:S(2)}) %collective-permute-start) | collective-permute-done | bytes 49184 | tf_op jit(solution)/shard_map/ppermute | solution.py:421
  6.8 0.9 copy-done.4
  7.7 5.5 %collective-permute-start.1 = (bf16[264,128]{1,0:T(8,128)(2,1)S(1)}, bf16[264,128]{1,0:T(8,128)(2,1)S(1)}, u32[]{:S(2)}, u32[]{:S(2)}) collective-permute-start(bf16[264,128]{1,0:T(8,128)(2,1)S(1)} %first_kernel.1.refs_0_), channel_id=1, source_target_pairs={{0,48},{8,56},{16,32},{24,40},{32,16},{40,24},{48,0},{56,8},{1,49}... | collective-permute-start | bytes 202760 | tf_op jit(solution)/shard_map/ppermute | solution.py:23
  13.2 3.9 %collective-permute-done.1.refs_1_ = bf16[264,128]{1,0:T(8,128)(2,1)S(1)} collective-permute-done((bf16[264,128]{1,0:T(8,128)(2,1)S(1)}, bf16[264,128]{1,0:T(8,128)(2,1)S(1)}, u32[]{:S(2)}, u32[]{:S(2)}) %collective-permute-start.1) | collective-permute-done | bytes 67616 | tf_op jit(solution)/shard_map/ppermute | solution.py:23
  17.1 1.1 collective-permute-start.4
  18.2 1.7 %collective-permute-start.3 = (bf16[336,128]{1,0:T(8,128)(2,1)S(1)}, bf16[336,128]{1,0:T(8,128)(2,1)S(1)}, u32[]{:S(2)}, u32[]{:S(2)}) collective-permute-start(bf16[336,128]{1,0:T(8,128)(2,1)S(1)} %stage_kernel.1.refs_0_), channel_id=1, source_target_pairs={{0,16},{8,24},{16,0},{24,8},{32,48},{40,56},{48,32},{56,40},{1,17}... | collective-permute-start | bytes 258056 | tf_op jit(solution)/shard_map/ppermute | solution.py:23
  19.9 0.8 collective-permute-start.2
  20.7 0.1 subtract_dynamic-update-slice_fusion
  20.9 4.6 %collective-permute-done.4.refs_3_ = bf16[336,128]{1,0:T(8,128)(2,1)S(1)} collective-permute-done((bf16[336,128]{1,0:T(8,128)(2,1)S(1)}, bf16[336,128]{1,0:T(8,128)(2,1)S(1)}, u32[]{:S(2)}, u32[]{:S(2)}) %collective-permute-start.4) | collective-permute-done | bytes 86048 | tf_op jit(solution)/shard_map/ppermute | solution.py:23
  25.4 0.0 collective-permute-done.3.refs_2_
  25.4 0.0 collective-permute-done.2.refs_1_
  25.5 2.8 %collective-permute-start.7 = (bf16[480,128]{1,0:T(8,128)(2,1)S(1)}, bf16[480,128]{1,0:T(8,128)(2,1)S(1)}, u32[]{:S(2)}, u32[]{:S(2)}) collective-permute-start(bf16[480,128]{1,0:T(8,128)(2,1)S(1)} %get-tuple-element.41.refs_0_), channel_id=1, source_target_pairs={{0,6},{2,4},{4,2},{6,0},{1,7},{3,5},{5,3},{7,1},{8,14},{10,12},{12... | collective-permute-start | bytes 368648 | tf_op jit(solution)/shard_map/ppermute | solution.py:23
  28.3 0.8 collective-permute-start.6
  29.1 0.5 collective-permute-start.5
  29.7 0.1 convert_reduce_fusion
  29.8 3.1 %collective-permute-start.14 = (bf16[288,128]{1,0:T(8,128)(2,1)S(1)}, bf16[288,128]{1,0:T(8,128)(2,1)S(1)}, u32[]{:S(2)}, u32[]{:S(2)}) collective-permute-start(bf16[288,128]{1,0:T(8,128)(2,1)S(1)} %get-tuple-element.43.refs_0_), channel_id=1, source_target_pairs={{0,192},{64,128},{128,64},{192,0},{1,193},{65,129},{129,65},{193,1... | collective-permute-start | bytes 221192 | tf_op jit(solution)/shard_map/ppermute | solution.py:23
  32.9 0.6 collective-permute-start.13
  33.5 0.0 collective-permute-done.7.refs_3_
  33.5 1.1 collective-permute-start.12
  34.6 0.6 collective-permute-done.6.refs_2_
  35.2 0.0 collective-permute-done.5.refs_1_
  35.2 3.1 %collective-permute-start.10 = (f32[96,128]{1,0:T(8,128)S(1)}, f32[96,128]{1,0:T(8,128)S(1)}, u32[]{:S(2)}, u32[]{:S(2)}) collective-permute-start(f32[96,128]{1,0:T(8,128)S(1)} %add_add_fusion.1), channel_id=1, source_target_pairs={{0,192},{64,128},{128,64},{192,0},{1,193},{65,129},{129,65},{193,1... | collective-permute-start | bytes 147464 | tf_op jit(solution)/shard_map/ppermute | solution.py:23
  38.3 0.6 collective-permute-start.9
  39.0 0.0 collective-permute-done.14.refs_3_
  39.0 0.5 collective-permute-start.8
  39.4 0.0 collective-permute-done.13.refs_2_
  39.4 0.0 collective-permute-done.12.refs_1_
  39.5 0.9 collective-permute-start.16
  40.4 1.4 %collective-permute-start.15 = (bf16[1152,128]{1,0:T(8,128)(2,1)S(1)}, bf16[1152,128]{1,0:T(8,128)(2,1)S(1)}, u32[]{:S(2)}, u32[]{:S(2)}) collective-permute-start(bf16[1152,128]{1,0:T(8,128)(2,1)S(1)} %join_kernel.2.base0), channel_id=1, source_target_pairs={{0,64},{64,0},{128,192},{192,128},{1,65},{65,1},{129,193},{193,129... | collective-permute-start | bytes 884744 | tf_op jit(solution)/shard_map/ppermute | solution.py:23
  41.8 0.0 collective-permute-done.10
  41.8 2.7 %collective-permute-done.9 = f32[96,128]{1,0:T(8,128)S(1)} collective-permute-done((f32[96,128]{1,0:T(8,128)S(1)}, f32[96,128]{1,0:T(8,128)S(1)}, u32[]{:S(2)}, u32[]{:S(2)}) %collective-permute-start.9) | collective-permute-done | bytes 49184 | tf_op jit(solution)/shard_map/ppermute | solution.py:23
  44.5 0.0 collective-permute-done.8
  44.5 0.1 collective-permute-start.11
  44.6 1.2 %collective-permute-done.11.other_ref = f32[96,128]{1,0:T(8,128)S(1)} collective-permute-done((f32[96,128]{1,0:T(8,128)S(1)}, f32[96,128]{1,0:T(8,128)S(1)}, u32[]{:S(2)}, u32[]{:S(2)}) %collective-permute-start.11) | collective-permute-done | bytes 49184 | tf_op jit(solution)/shard_map/ppermute | solution.py:23
  45.9 2.1 %column_sum.1 = (f32[4,32,192]{2,1,0:T(8,128)S(1)}, f32[32,15,128]{2,1,0:T(8,128)}) custom-call(f32[96,128]{1,0:T(8,128)S(1)} %add_add_fusion.own_ref, f32[96,128]{1,0:T(8,128)S(1)} %collective-permute-done.11.other_ref, f32[32,32]{1,0:T(8,128)S(1)} %copy-done.5, bf16[768,1536]{1,0:T(8,128)(2,1)S(1)} %copy-done, f32[96,128]{1,0:T(8,128)S(1)} %fusion.vec_ref), custom_call_target="tpu_custom_call" | custom-call | tf_op jit(solution)/shard_map/column_sum/pallas_call | solution.py:233
  48.0 0.0 collective-permute-done.16.rest1
  48.0 0.0 collective-permute-done.15.base1
  48.0 0.7 copy-done.8
  48.8 10.3 %all-to-all-start = ((f32[32,15,128]{2,1,0:T(8,128)}), f32[32,15,128]{2,1,0:T(8,128)S(1)}, u32[]{:S(2)}, u32[]{:S(2)}) async-start(f32[32,15,128]{2,1,0:T(8,128)} %get-tuple-element.50), calls=%async_computation | async-start | bytes 524288 | tf_op jit(solution)/shard_map/all_to_all | solution.py:453
  59.1 2.9 %collective-permute-start.20 = (bf16[1152,128]{1,0:T(8,128)(2,1)S(1)}, bf16[1152,128]{1,0:T(8,128)(2,1)S(1)}, u32[]{:S(2)}, u32[]{:S(2)}) collective-permute-start(bf16[1152,128]{1,0:T(8,128)(2,1)S(1)} %join_kernel.3.rest0), channel_id=1, source_target_pairs={{0,6},{2,4},{4,2},{6,0},{1,7},{3,5},{5,3},{7,1},{8,14},{10,12},{12... | collective-permute-start | bytes 884744 | tf_op jit(solution)/shard_map/ppermute | solution.py:23
  62.0 0.9 collective-permute-start.19
  62.9 2.2 %collective-permute-start.18 = (bf16[1152,128]{1,0:T(8,128)(2,1)S(1)}, bf16[1152,128]{1,0:T(8,128)(2,1)S(1)}, u32[]{:S(2)}, u32[]{:S(2)}) collective-permute-start(bf16[1152,128]{1,0:T(8,128)(2,1)S(1)} %join_kernel.2.base0), channel_id=1, source_target_pairs={{0,192},{64,128},{128,64},{192,0},{1,193},{65,129},{129,65},{193,1... | collective-permute-start | bytes 884744 | tf_op jit(solution)/shard_map/ppermute | solution.py:23
  65.1 0.9 collective-permute-start.17
  66.0 5.2 %all-to-all-done = f32[32,15,128]{2,1,0:T(8,128)S(1)} async-done(((f32[32,15,128]{2,1,0:T(8,128)}), f32[32,15,128]{2,1,0:T(8,128)S(1)}, u32[]{:S(2)}, u32[]{:S(2)}) %all-to-all-start) | async-done | bytes 245792 | tf_op jit(solution)/shard_map/all_to_all | solution.py:453
  71.2 6.2 %collective-permute-done.20.rest3 = bf16[1152,128]{1,0:T(8,128)(2,1)S(1)} collective-permute-done((bf16[1152,128]{1,0:T(8,128)(2,1)S(1)}, bf16[1152,128]{1,0:T(8,128)(2,1)S(1)}, u32[]{:S(2)}, u32[]{:S(2)}) %collective-permute-start.20) | collective-permute-done | bytes 294944 | tf_op jit(solution)/shard_map/ppermute | solution.py:23
  77.4 0.0 collective-permute-done.19.rest2
  77.4 0.4 collective-permute-done.18.base3
  77.8 0.0 collective-permute-done.17.base2
  77.8 1.9 %collective-permute-start.23 = (f32[15,128]{1,0:T(8,128)S(1)}, f32[15,128]{1,0:T(8,128)S(1)}, u32[]{:S(2)}, u32[]{:S(2)}) collective-permute-start(f32[15,128]{1,0:T(8,128)S(1)} %reduce_sum.9.refs_0_), channel_id=1, source_target_pairs={{0,192},{64,128},{128,64},{192,0},{1,193},{65,129},{129,65},{193,1... | collective-permute-start | bytes 23048 | tf_op jit(solution)/shard_map/ppermute | solution.py:23
  79.7 0.5 collective-permute-start.22
  80.2 1.8 %collective-permute-start.21 = (f32[15,128]{1,0:T(8,128)S(1)}, f32[15,128]{1,0:T(8,128)S(1)}, u32[]{:S(2)}, u32[]{:S(2)}) collective-permute-start(f32[15,128]{1,0:T(8,128)S(1)} %reduce_sum.9.refs_0_), channel_id=1, source_target_pairs={{0,64},{64,0},{128,192},{192,128},{1,65},{65,1},{129,193},{193,129... | collective-permute-start | bytes 23048 | tf_op jit(solution)/shard_map/ppermute | solution.py:23
  82.0 0.8 collective-permute-done.23.refs_3_
  82.8 2.1 %collective-permute-done.22.refs_2_ = f32[15,128]{1,0:T(8,128)S(1)} collective-permute-done((f32[15,128]{1,0:T(8,128)S(1)}, f32[15,128]{1,0:T(8,128)S(1)}, u32[]{:S(2)}, u32[]{:S(2)}) %collective-permute-start.22) | collective-permute-done | bytes 7712 | tf_op jit(solution)/shard_map/ppermute | solution.py:23
  84.9 0.7 repeat.1
  85.6 9.5 %all-to-all-start.1 = ((f32[32,15,128]{2,1,0:T(8,128)}), f32[32,15,128]{2,1,0:T(8,128)S(1)}, u32[]{:S(2)}, u32[]{:S(2)}) async-start(f32[32,15,128]{2,1,0:T(8,128)} %repeat.1), calls=%async_computation.1 | async-start | bytes 524288 | tf_op jit(solution)/shard_map/all_to_all | solution.py:456
  95.1 0.7 pad_add_fusion.where
  95.7 0.7 dynamic-slice_bitcast_fusion.own_basis_ref
  96.4 9.5 %all-to-all-done.1.piece_ref = f32[32,15,128]{2,1,0:T(8,128)S(1)} async-done(((f32[32,15,128]{2,1,0:T(8,128)}), f32[32,15,128]{2,1,0:T(8,128)S(1)}, u32[]{:S(2)}, u32[]{:S(2)}) %all-to-all-start.1) | async-done | bytes 245792 | tf_op jit(solution)/shard_map/all_to_all | solution.py:456
  105.9 0.7 copy-done.6
  106.6 7.6 %apply.1 = (bf16[768,1536]{1,0:T(8,128)(2,1)}, bf16[768,1536]{1,0:T(8,128)(2,1)}, f32[6,1536]{1,0:T(8,128)}, f32[6,1536]{1,0:T(8,128)}, bf16[42,128]{1,0:T(8,128...) custom-call(s32[3]{0:T(128)} %pad_add_fusion.where, f32[32,6]{1,0:T(8,128)} %dynamic-slice_bitcast_fusion.own_basis_ref, ...), custom_call_target="tpu_custom_call" | custom-call | tf_op jit(solution)/shard_map/apply/pallas_call | solution.py:353
  (38 shorter events, 0.3 us)
Async XLA Ops:
  0.6 20.1 %copy-start.14 = (f32[42]{0:T(128)S(1)}, f32[42]{0:T(128)}, u32[]{:S(2)}) copy-start(f32[42]{0:T(128)} %param.16) | copy-start | bytes 508
  0.6 20.1 %copy-start.15 = (f32[42]{0:T(128)S(1)}, f32[42]{0:T(128)}, u32[]{:S(2)}) copy-start(f32[42]{0:T(128)} %param.17) | copy-start | bytes 508
  0.7 29.0 %copy-start.13 = (bf16[1,5376]{1,0:T(2,128)(2,1)S(1)}, bf16[1,5376]{1,0:T(2,128)(2,1)}, u32[]{:S(2)}) copy-start(bf16[1,5376]{1,0:T(2,128)(2,1)} %param.15) | copy-start | bytes 32260
  0.7 45.2 %copy-start.5 = (f32[32,32]{1,0:T(8,128)S(1)}, f32[32,32]{1,0:T(8,128)}, u32[]{:S(2)}) copy-start(f32[32,32]{1,0:T(8,128)} %gram_ref.1) | copy-start | bytes 12292
  5.3 40.6 %copy-start = (bf16[768,1536]{1,0:T(8,128)(2,1)S(1)}, bf16[768,1536]{1,0:T(8,128)(2,1)}, u32[]{:S(2)}) copy-start(bf16[768,1536]{1,0:T(8,128)(2,1)} %get-tuple-element.46.merged_ref) | copy-start | bytes 7077892
  5.3 1.5 %collective-permute-start = (f32[96,128]{1,0:T(8,128)}, f32[96,128]{1,0:T(8,128)S(1)}, u32[]{:S(2)}, u32[]{:S(2)}) collective-permute-start(f32[96,128]{1,0:T(8,128)} %get-tuple-element.40), channel_id=1, source_target_pairs={{0,1},{1,0},{2,3},{3,2},{4,5},{5,4},{6,7},{7,6},{8,9},{9,8},{10,11... | collective-permute-start | bytes 147464 | tf_op jit(solution)/shard_map/ppermute | solution.py:421
  6.8 0.9 copy-start.4
  7.7 9.4 %collective-permute-start.1 = (bf16[264,128]{1,0:T(8,128)(2,1)S(1)}, bf16[264,128]{1,0:T(8,128)(2,1)S(1)}, u32[]{:S(2)}, u32[]{:S(2)}) collective-permute-start(bf16[264,128]{1,0:T(8,128)(2,1)S(1)} %first_kernel.1.refs_0_), channel_id=1, source_target_pairs={{0,48},{8,56},{16,32},{24,40},{32,16},{40,24},{48,0},{56,8},{1,49}... | collective-permute-start | bytes 202760 | tf_op jit(solution)/shard_map/ppermute | solution.py:23
  17.1 8.3 %collective-permute-start.4 = (bf16[336,128]{1,0:T(8,128)(2,1)S(1)}, bf16[336,128]{1,0:T(8,128)(2,1)S(1)}, u32[]{:S(2)}, u32[]{:S(2)}) collective-permute-start(bf16[336,128]{1,0:T(8,128)(2,1)S(1)} %stage_kernel.1.refs_0_), channel_id=1, source_target_pairs={{0,24},{8,16},{16,8},{24,0},{32,56},{40,48},{48,40},{56,32},{1,25}... | collective-permute-start | bytes 258056 | tf_op jit(solution)/shard_map/ppermute | solution.py:23
  18.2 7.2 %collective-permute-start.3 = (bf16[336,128]{1,0:T(8,128)(2,1)S(1)}, bf16[336,128]{1,0:T(8,128)(2,1)S(1)}, u32[]{:S(2)}, u32[]{:S(2)}) collective-permute-start(bf16[336,128]{1,0:T(8,128)(2,1)S(1)} %stage_kernel.1.refs_0_), channel_id=1, source_target_pairs={{0,16},{8,24},{16,0},{24,8},{32,48},{40,56},{48,32},{56,40},{1,17}... | collective-permute-start | bytes 258056 | tf_op jit(solution)/shard_map/ppermute | solution.py:23
  19.9 5.5 %collective-permute-start.2 = (bf16[336,128]{1,0:T(8,128)(2,1)S(1)}, bf16[336,128]{1,0:T(8,128)(2,1)S(1)}, u32[]{:S(2)}, u32[]{:S(2)}) collective-permute-start(bf16[336,128]{1,0:T(8,128)(2,1)S(1)} %stage_kernel.1.refs_0_), channel_id=1, source_target_pairs={{0,8},{8,0},{16,24},{24,16},{32,40},{40,32},{48,56},{56,48},{1,9},... | collective-permute-start | bytes 258056 | tf_op jit(solution)/shard_map/ppermute | solution.py:23
  25.5 8.0 %collective-permute-start.7 = (bf16[480,128]{1,0:T(8,128)(2,1)S(1)}, bf16[480,128]{1,0:T(8,128)(2,1)S(1)}, u32[]{:S(2)}, u32[]{:S(2)}) collective-permute-start(bf16[480,128]{1,0:T(8,128)(2,1)S(1)} %get-tuple-element.41.refs_0_), channel_id=1, source_target_pairs={{0,6},{2,4},{4,2},{6,0},{1,7},{3,5},{5,3},{7,1},{8,14},{10,12},{12... | collective-permute-start | bytes 368648 | tf_op jit(solution)/shard_map/ppermute | solution.py:23
  28.3 6.9 %collective-permute-start.6 = (bf16[480,128]{1,0:T(8,128)(2,1)S(1)}, bf16[480,128]{1,0:T(8,128)(2,1)S(1)}, u32[]{:S(2)}, u32[]{:S(2)}) collective-permute-start(bf16[480,128]{1,0:T(8,128)(2,1)S(1)} %get-tuple-element.41.refs_0_), channel_id=1, source_target_pairs={{0,4},{2,6},{4,0},{6,2},{1,5},{3,7},{5,1},{7,3},{8,12},{10,14},{12... | collective-permute-start | bytes 368648 | tf_op jit(solution)/shard_map/ppermute | solution.py:23
  29.1 6.1 %collective-permute-start.5 = (bf16[480,128]{1,0:T(8,128)(2,1)S(1)}, bf16[480,128]{1,0:T(8,128)(2,1)S(1)}, u32[]{:S(2)}, u32[]{:S(2)}) collective-permute-start(bf16[480,128]{1,0:T(8,128)(2,1)S(1)} %get-tuple-element.41.refs_0_), channel_id=1, source_target_pairs={{0,2},{2,0},{4,6},{6,4},{1,3},{3,1},{5,7},{7,5},{8,10},{10,8},{12,... | collective-permute-start | bytes 368648 | tf_op jit(solution)/shard_map/ppermute | solution.py:23
  29.8 9.2 %collective-permute-start.14 = (bf16[288,128]{1,0:T(8,128)(2,1)S(1)}, bf16[288,128]{1,0:T(8,128)(2,1)S(1)}, u32[]{:S(2)}, u32[]{:S(2)}) collective-permute-start(bf16[288,128]{1,0:T(8,128)(2,1)S(1)} %get-tuple-element.43.refs_0_), channel_id=1, source_target_pairs={{0,192},{64,128},{128,64},{192,0},{1,193},{65,129},{129,65},{193,1... | collective-permute-start | bytes 221192 | tf_op jit(solution)/shard_map/ppermute | solution.py:23
  32.9 6.6 %collective-permute-start.13 = (bf16[288,128]{1,0:T(8,128)(2,1)S(1)}, bf16[288,128]{1,0:T(8,128)(2,1)S(1)}, u32[]{:S(2)}, u32[]{:S(2)}) collective-permute-start(bf16[288,128]{1,0:T(8,128)(2,1)S(1)} %get-tuple-element.43.refs_0_), channel_id=1, source_target_pairs={{0,128},{64,192},{128,0},{192,64},{1,129},{65,193},{129,1},{193,65... | collective-permute-start | bytes 221192 | tf_op jit(solution)/shard_map/ppermute | solution.py:23
  33.5 5.9 %collective-permute-start.12 = (bf16[288,128]{1,0:T(8,128)(2,1)S(1)}, bf16[288,128]{1,0:T(8,128)(2,1)S(1)}, u32[]{:S(2)}, u32[]{:S(2)}) collective-permute-start(bf16[288,128]{1,0:T(8,128)(2,1)S(1)} %get-tuple-element.43.refs_0_), channel_id=1, source_target_pairs={{0,64},{64,0},{128,192},{192,128},{1,65},{65,1},{129,193},{193,129... | collective-permute-start | bytes 221192 | tf_op jit(solution)/shard_map/ppermute | solution.py:23
  35.2 6.6 %collective-permute-start.10 = (f32[96,128]{1,0:T(8,128)S(1)}, f32[96,128]{1,0:T(8,128)S(1)}, u32[]{:S(2)}, u32[]{:S(2)}) collective-permute-start(f32[96,128]{1,0:T(8,128)S(1)} %add_add_fusion.1), channel_id=1, source_target_pairs={{0,192},{64,128},{128,64},{192,0},{1,193},{65,129},{129,65},{193,1... | collective-permute-start | bytes 147464 | tf_op jit(solution)/shard_map/ppermute | solution.py:23
  38.3 6.2 %collective-permute-start.9 = (f32[96,128]{1,0:T(8,128)S(1)}, f32[96,128]{1,0:T(8,128)S(1)}, u32[]{:S(2)}, u32[]{:S(2)}) collective-permute-start(f32[96,128]{1,0:T(8,128)S(1)} %add_add_fusion.1), channel_id=1, source_target_pairs={{0,128},{64,192},{128,0},{192,64},{1,129},{65,193},{129,1},{193,65... | collective-permute-start | bytes 147464 | tf_op jit(solution)/shard_map/ppermute | solution.py:23
  39.0 5.6 %collective-permute-start.8 = (f32[96,128]{1,0:T(8,128)S(1)}, f32[96,128]{1,0:T(8,128)S(1)}, u32[]{:S(2)}, u32[]{:S(2)}) collective-permute-start(f32[96,128]{1,0:T(8,128)S(1)} %add_add_fusion.1), channel_id=1, source_target_pairs={{0,64},{64,0},{128,192},{192,128},{1,65},{65,1},{129,193},{193,129... | collective-permute-start | bytes 147464 | tf_op jit(solution)/shard_map/ppermute | solution.py:23
  39.4 46.1 %copy-start.2 = (bf16[1152,128]{1,0:T(8,128)(2,1)}, bf16[1152,128]{1,0:T(8,128)(2,1)S(1)}, u32[]{:S(2)}) copy-start(bf16[1152,128]{1,0:T(8,128)(2,1)S(1)} %join_kernel.3.rest0) | copy-start | bytes 884740
  39.5 8.6 %collective-permute-start.16 = (bf16[1152,128]{1,0:T(8,128)(2,1)S(1)}, bf16[1152,128]{1,0:T(8,128)(2,1)S(1)}, u32[]{:S(2)}, u32[]{:S(2)}) collective-permute-start(bf16[1152,128]{1,0:T(8,128)(2,1)S(1)} %join_kernel.3.rest0), channel_id=1, source_target_pairs={{0,2},{2,0},{4,6},{6,4},{1,3},{3,1},{5,7},{7,5},{8,10},{10,8},{12,... | collective-permute-start | bytes 884744 | tf_op jit(solution)/shard_map/ppermute | solution.py:23
  40.3 65.5 %copy-start.1 = (bf16[1152,128]{1,0:T(8,128)(2,1)}, bf16[1152,128]{1,0:T(8,128)(2,1)S(1)}, u32[]{:S(2)}) copy-start(bf16[1152,128]{1,0:T(8,128)(2,1)S(1)} %join_kernel.2.base0) | copy-start | bytes 884740
  40.4 7.7 %collective-permute-start.15 = (bf16[1152,128]{1,0:T(8,128)(2,1)S(1)}, bf16[1152,128]{1,0:T(8,128)(2,1)S(1)}, u32[]{:S(2)}, u32[]{:S(2)}) collective-permute-start(bf16[1152,128]{1,0:T(8,128)(2,1)S(1)} %join_kernel.2.base0), channel_id=1, source_target_pairs={{0,64},{64,0},{128,192},{192,128},{1,65},{65,1},{129,193},{193,129... | collective-permute-start | bytes 884744 | tf_op jit(solution)/shard_map/ppermute | solution.py:23
  44.5 1.3 %collective-permute-start.11 = (f32[96,128]{1,0:T(8,128)S(1)}, f32[96,128]{1,0:T(8,128)S(1)}, u32[]{:S(2)}, u32[]{:S(2)}) collective-permute-start(f32[96,128]{1,0:T(8,128)S(1)} %add_add_fusion.own_ref), channel_id=1, source_target_pairs={{0,1},{1,0},{2,3},{3,2},{4,5},{5,4},{6,7},{7,6},{8,9},{9,8},{10,11... | collective-permute-start | bytes 147464 | tf_op jit(solution)/shard_map/ppermute | solution.py:23
  48.0 57.9 %copy-start.3 = (f32[4,32,192]{2,1,0:T(8,128)}, f32[4,32,192]{2,1,0:T(8,128)S(1)}, u32[]{:S(2)}) copy-start(f32[4,32,192]{2,1,0:T(8,128)S(1)} %get-tuple-element.48.basis_hbm) | copy-start | bytes 294916
  48.0 57.9 %copy-start.7 = (bf16[1152,128]{1,0:T(8,128)(2,1)}, bf16[1152,128]{1,0:T(8,128)(2,1)S(1)}, u32[]{:S(2)}) copy-start(bf16[1152,128]{1,0:T(8,128)(2,1)S(1)} %collective-permute-done.16.rest1) | copy-start | bytes 884740
  48.0 0.7 copy-start.8
  48.8 22.4 %all-to-all-start = ((f32[32,15,128]{2,1,0:T(8,128)}), f32[32,15,128]{2,1,0:T(8,128)S(1)}, u32[]{:S(2)}, u32[]{:S(2)}) async-start(f32[32,15,128]{2,1,0:T(8,128)} %get-tuple-element.50), calls=%async_computation | async-start | bytes 524288 | tf_op jit(solution)/shard_map/all_to_all | solution.py:453
  59.1 18.3 %collective-permute-start.20 = (bf16[1152,128]{1,0:T(8,128)(2,1)S(1)}, bf16[1152,128]{1,0:T(8,128)(2,1)S(1)}, u32[]{:S(2)}, u32[]{:S(2)}) collective-permute-start(bf16[1152,128]{1,0:T(8,128)(2,1)S(1)} %join_kernel.3.rest0), channel_id=1, source_target_pairs={{0,6},{2,4},{4,2},{6,0},{1,7},{3,5},{5,3},{7,1},{8,14},{10,12},{12... | collective-permute-start | bytes 884744 | tf_op jit(solution)/shard_map/ppermute | solution.py:23
  62.0 15.4 %collective-permute-start.19 = (bf16[1152,128]{1,0:T(8,128)(2,1)S(1)}, bf16[1152,128]{1,0:T(8,128)(2,1)S(1)}, u32[]{:S(2)}, u32[]{:S(2)}) collective-permute-start(bf16[1152,128]{1,0:T(8,128)(2,1)S(1)} %join_kernel.3.rest0), channel_id=1, source_target_pairs={{0,4},{2,6},{4,0},{6,2},{1,5},{3,7},{5,1},{7,3},{8,12},{10,14},{12... | collective-permute-start | bytes 884744 | tf_op jit(solution)/shard_map/ppermute | solution.py:23
  62.9 14.9 %collective-permute-start.18 = (bf16[1152,128]{1,0:T(8,128)(2,1)S(1)}, bf16[1152,128]{1,0:T(8,128)(2,1)S(1)}, u32[]{:S(2)}, u32[]{:S(2)}) collective-permute-start(bf16[1152,128]{1,0:T(8,128)(2,1)S(1)} %join_kernel.2.base0), channel_id=1, source_target_pairs={{0,192},{64,128},{128,64},{192,0},{1,193},{65,129},{129,65},{193,1... | collective-permute-start | bytes 884744 | tf_op jit(solution)/shard_map/ppermute | solution.py:23
  65.1 12.7 %collective-permute-start.17 = (bf16[1152,128]{1,0:T(8,128)(2,1)S(1)}, bf16[1152,128]{1,0:T(8,128)(2,1)S(1)}, u32[]{:S(2)}, u32[]{:S(2)}) collective-permute-start(bf16[1152,128]{1,0:T(8,128)(2,1)S(1)} %join_kernel.2.base0), channel_id=1, source_target_pairs={{0,128},{64,192},{128,0},{192,64},{1,129},{65,193},{129,1},{193,65... | collective-permute-start | bytes 884744 | tf_op jit(solution)/shard_map/ppermute | solution.py:23
  77.4 28.5 %copy-start.9 = (bf16[1152,128]{1,0:T(8,128)(2,1)}, bf16[1152,128]{1,0:T(8,128)(2,1)S(1)}, u32[]{:S(2)}) copy-start(bf16[1152,128]{1,0:T(8,128)(2,1)S(1)} %collective-permute-done.20.rest3) | copy-start | bytes 884740
  77.4 28.5 %copy-start.10 = (bf16[1152,128]{1,0:T(8,128)(2,1)}, bf16[1152,128]{1,0:T(8,128)(2,1)S(1)}, u32[]{:S(2)}) copy-start(bf16[1152,128]{1,0:T(8,128)(2,1)S(1)} %collective-permute-done.19.rest2) | copy-start | bytes 884740
  77.8 28.1 %copy-start.11 = (bf16[1152,128]{1,0:T(8,128)(2,1)}, bf16[1152,128]{1,0:T(8,128)(2,1)S(1)}, u32[]{:S(2)}) copy-start(bf16[1152,128]{1,0:T(8,128)(2,1)S(1)} %collective-permute-done.18.base3) | copy-start | bytes 884740
  77.8 28.1 %copy-start.12 = (bf16[1152,128]{1,0:T(8,128)(2,1)}, bf16[1152,128]{1,0:T(8,128)(2,1)S(1)}, u32[]{:S(2)}) copy-start(bf16[1152,128]{1,0:T(8,128)(2,1)S(1)} %collective-permute-done.17.base2) | copy-start | bytes 884740
  77.8 4.9 %collective-permute-start.23 = (f32[15,128]{1,0:T(8,128)S(1)}, f32[15,128]{1,0:T(8,128)S(1)}, u32[]{:S(2)}, u32[]{:S(2)}) collective-permute-start(f32[15,128]{1,0:T(8,128)S(1)} %reduce_sum.9.refs_0_), channel_id=1, source_target_pairs={{0,192},{64,128},{128,64},{192,0},{1,193},{65,129},{129,65},{193,1... | collective-permute-start | bytes 23048 | tf_op jit(solution)/shard_map/ppermute | solution.py:23
  79.7 5.2 %collective-permute-start.22 = (f32[15,128]{1,0:T(8,128)S(1)}, f32[15,128]{1,0:T(8,128)S(1)}, u32[]{:S(2)}, u32[]{:S(2)}) collective-permute-start(f32[15,128]{1,0:T(8,128)S(1)} %reduce_sum.9.refs_0_), channel_id=1, source_target_pairs={{0,128},{64,192},{128,0},{192,64},{1,129},{65,193},{129,1},{193,65... | collective-permute-start | bytes 23048 | tf_op jit(solution)/shard_map/ppermute | solution.py:23
  80.2 4.6 %collective-permute-start.21 = (f32[15,128]{1,0:T(8,128)S(1)}, f32[15,128]{1,0:T(8,128)S(1)}, u32[]{:S(2)}, u32[]{:S(2)}) collective-permute-start(f32[15,128]{1,0:T(8,128)S(1)} %reduce_sum.9.refs_0_), channel_id=1, source_target_pairs={{0,64},{64,0},{128,192},{192,128},{1,65},{65,1},{129,193},{193,129... | collective-permute-start | bytes 23048 | tf_op jit(solution)/shard_map/ppermute | solution.py:23
  85.6 20.3 %all-to-all-start.1 = ((f32[32,15,128]{2,1,0:T(8,128)}), f32[32,15,128]{2,1,0:T(8,128)S(1)}, u32[]{:S(2)}, u32[]{:S(2)}) async-start(f32[32,15,128]{2,1,0:T(8,128)} %repeat.1), calls=%async_computation.1 | async-start | bytes 524288 | tf_op jit(solution)/shard_map/all_to_all | solution.py:456
  105.9 0.7 copy-start.6
